TPU v7x, 32 devices: a whole 2x2x4 slice. The times are simulated.
32 devices in a mesh: wide: 8 (over z, x), narrow: 4 (over y, core).
Axes of the slice: x: 2, y: 2, z: 4, core: 2. Of those that a mesh axis runs over, the one named last changes fastest.
Arguments:
- tokens: bfloat16 [65536, 768], P(('wide', 'narrow')), may hold values from -6 to 6
- timestep: int32 [64], P(('wide', 'narrow')), may hold values from 0 to 999
- span_start: int32 [64], P(('wide', 'narrow')), may hold values from 0 to 511
- span_length: int32 [64], P(('wide', 'narrow')), may hold values from 1 to 512
- mask_embed: bfloat16 [768], P('narrow'), may hold values from -6 to 6
- ada_weight: bfloat16 [128, 4608], P(None, 'narrow'), may hold values from -0.5 to 0.5
- ada_bias: bfloat16 [4608], P('narrow'), may hold values from -3 to 3
- norm_first: bfloat16 [768], P('narrow'), may hold values from 0.099609375 to 1.8984375
- query_key_value_weight: bfloat16 [768, 2304], P('narrow'), may hold values from -0.21875 to 0.21875
- output_weight: bfloat16 [768, 768], P('narrow'), may hold values from -1.25 to 1.25
- norm_second: bfloat16 [768], P('narrow'), may hold values from 0.099609375 to 1.8984375
- up_projection_weight: bfloat16 [768, 3072], P('narrow'), may hold values from -0.21875 to 0.21875
- up_projection_bias: bfloat16 [3072], P('narrow'), may hold values from -3 to 3
- down_projection_weight: bfloat16 [3072, 768], P('narrow'), may hold values from -0.109375 to 0.109375
- down_projection_bias: bfloat16 [768], P('narrow'), may hold values from -3 to 3
- cotangent: bfloat16 [65536, 768], P(('wide', 'narrow')), may hold values from -6 to 6
Outputs:
- block_out: bfloat16 [65536, 768], P(('wide', 'narrow'))
- grad_tokens: float32 [65536, 768], P(('wide', 'narrow'))
- grad_mask_embed: float32 [768], P('narrow')
- grad_ada_weight: float32 [128, 4608], P(None, 'narrow')
- grad_ada_bias: float32 [4608], P('narrow')
- grad_norm_first: float32 [768], P('narrow')
- grad_qkv_weight: float32 [768, 2304], P('narrow')
- grad_out_weight: float32 [768, 768], P('narrow')
- grad_norm_second: float32 [768], P('narrow')
- grad_up_weight: float32 [768, 3072], P('narrow')
- grad_up_bias: float32 [3072], P('narrow')
- grad_down_weight: float32 [3072, 768], P('narrow')
- grad_down_bias: float32 [768], P('narrow')
Inputs may be any that keep to these rules, and one draw needn't show every extreme that they name: `timestep`: one diffusion step index per sequence, below 1000. `span_start`: the masked span starts in the first half of its sequence. `span_length`: the masked span holds at least one position and ends inside its sequence.
All inputs are finite; a program needn't handle non-finite values.
Results may differ from a plain program's by a relative error of at most 0.012.
The roundings to bfloat16 on the way count: a program that leaves them out, or rounds other values in their place, can miss the bound.
Values may be sent and summed in bfloat16 or wider, within the bound.
A program may use at most 320 MiB of HBM per device.

v0:
```python
import math

import jax
import jax.numpy as jnp
from jax import lax
from jax.sharding import PartitionSpec as P

HEAD = 64
MICRO = 2


EPSILON = 1e-05
FULL_PRECISION = lax.Precision.HIGHEST


def time_features(step_ids, feature_count):
    halfway = feature_count // 2
    spacing = jnp.exp(-math.log(10000.0) * jnp.arange(halfway, dtype=jnp.float32) / halfway)
    angles = step_ids.astype(jnp.float32)[:, None] * spacing[None, :]
    wave_rows = jnp.concatenate([jnp.cos(angles), jnp.sin(angles)], axis=-1)
    return jax.nn.silu(wave_rows)


def rotary_tables(seq_length, head_width):
    halfway = head_width // 2
    spacing = jnp.exp(-math.log(10000.0) * jnp.arange(halfway, dtype=jnp.float32) / halfway)
    angles = jnp.arange(seq_length, dtype=jnp.float32)[:, None] * spacing[None, :]
    cosine = jnp.concatenate([jnp.cos(angles), jnp.cos(angles)], axis=-1)[:, None, :]
    sine_table = jnp.concatenate([jnp.sin(angles), jnp.sin(angles)], axis=-1)[:, None, :]
    return (cosine, sine_table)


def rotate(vectors, cosine, sine_table):
    halfway = vectors.shape[-1] // 2
    turned = jnp.concatenate([-vectors[..., halfway:], vectors[..., :halfway]], axis=-1)
    return vectors * cosine + turned * sine_table


def rotate_back(gradient, cosine, sine_table):
    halfway = gradient.shape[-1] // 2
    scaled = gradient * sine_table
    turned = jnp.concatenate([scaled[..., halfway:], -scaled[..., :halfway]], axis=-1)
    return gradient * cosine + turned


def modulate(hidden, norm_gain, shift_vec, scale_vec):
    centre = hidden - jnp.mean(hidden, axis=-1, keepdims=True)
    spread = jnp.mean(centre * centre, axis=-1, keepdims=True)
    return centre * lax.rsqrt(spread + EPSILON) * norm_gain * (1.0 + scale_vec) + shift_vec


def gelu_tanh(hidden):
    return jax.nn.gelu(hidden, approximate=True)


def span_mask(starts, lengths, seq_length):
    positions = jnp.arange(seq_length, dtype=jnp.int32)[None, :]
    return (positions >= starts[:, None]) & (positions < starts[:, None] + lengths[:, None])


def contract_rows(leading, trailing):
    return lax.dot_general(
        leading, trailing, (((0,), (0,)), ((), ())), preferred_element_type=jnp.float32
    )


def times_transposed(leading, trailing):
    return lax.dot_general(
        leading, trailing, (((1,), (1,)), ((), ())), preferred_element_type=jnp.float32
    )


def attend(queries, keys_all, values_all):
    seq_length, head_count, head_width = queries.shape[1:]
    block_rows = min(512, seq_length)
    block_count = seq_length // block_rows
    factor = 1.0 / math.sqrt(head_width)

    def per_sequence(operands):
        query_seq, keys_seq, values_seq = operands
        query_blocks = query_seq.reshape(block_count, block_rows, head_count, head_width)

        def per_block(query_block):
            scores = (
                jnp.einsum(
                    "qhd,khd->hqk", query_block, keys_seq, preferred_element_type=jnp.float32
                )
                * factor
            )
            row_max = jnp.max(scores, axis=-1, keepdims=True)
            exponent = jnp.exp(scores - row_max)
            denominator = jnp.sum(exponent, axis=-1, keepdims=True)
            probs_low = (exponent / denominator).astype(jnp.bfloat16)
            mixed_values = jnp.einsum(
                "hqk,khd->qhd", probs_low, values_seq, preferred_element_type=jnp.float32
            )
            return (mixed_values.astype(jnp.bfloat16), (row_max + jnp.log(denominator))[..., 0])

        mixture_blocks, log_totals = lax.map(per_block, query_blocks)
        return (mixture_blocks.reshape(seq_length, head_count, head_width), log_totals)

    return lax.map(per_sequence, (queries, keys_all, values_all))


def attend_back(queries, keys_all, values_all, d_mixture, log_totals):
    seq_length, head_count, head_width = queries.shape[1:]
    block_rows = min(512, seq_length)
    block_count = seq_length // block_rows
    factor = 1.0 / math.sqrt(head_width)

    def per_sequence(operands):
        query_seq, keys_seq, values_seq, grad_seq, total_seq = operands
        query_blocks = query_seq.reshape(block_count, block_rows, head_count, head_width)
        grad_blocks = grad_seq.reshape(block_count, block_rows, head_count, head_width)

        def per_block(running, block_items):
            keys_grad, values_grad = running
            query_block, grad_block, total_block = block_items
            scores = (
                jnp.einsum(
                    "qhd,khd->hqk", query_block, keys_seq, preferred_element_type=jnp.float32
                )
                * factor
            )
            probs = jnp.exp(scores - total_block[..., None])
            d_probs = jnp.einsum(
                "qhd,khd->hqk", grad_block, values_seq, preferred_element_type=jnp.float32
            )
            values_grad = values_grad + jnp.einsum(
                "hqk,qhd->khd",
                probs.astype(jnp.bfloat16),
                grad_block,
                preferred_element_type=jnp.float32,
            )
            d_scores = (
                probs * (d_probs - jnp.sum(d_probs * probs, axis=-1, keepdims=True))
            ).astype(jnp.bfloat16)
            query_grad = (
                jnp.einsum("hqk,khd->qhd", d_scores, keys_seq, preferred_element_type=jnp.float32)
                * factor
            )
            keys_grad = (
                keys_grad
                + jnp.einsum(
                    "hqk,qhd->khd", d_scores, query_block, preferred_element_type=jnp.float32
                )
                * factor
            )
            return ((keys_grad, values_grad), query_grad)

        zeros_init = jnp.zeros((seq_length, head_count, head_width), jnp.float32)
        (keys_grad, values_grad), query_grads = lax.scan(
            per_block, (zeros_init, zeros_init), (query_blocks, grad_blocks, total_seq)
        )
        return (query_grads.reshape(seq_length, head_count, head_width), keys_grad, values_grad)

    return lax.map(per_sequence, (queries, keys_all, values_all, d_mixture, log_totals))


def forward_pass(weights, token_rows, step_ids, starts, lengths):
    (
        mask_embed,
        ada_weight,
        ada_bias,
        norm_first,
        query_key_value_weight,
        output_weight,
        norm_second,
        up_projection_weight,
        up_projection_bias,
        down_projection_weight,
        down_projection_bias,
    ) = weights
    seq_count = step_ids.shape[0]
    row_count, model_width = token_rows.shape
    seq_length = row_count // seq_count
    head_count = model_width // HEAD
    features = time_features(step_ids, ada_weight.shape[0])
    modulation = (
        jnp.dot(features, ada_weight.astype(jnp.float32), precision=FULL_PRECISION)
        + ada_bias.astype(jnp.float32)
    ).reshape(seq_count, 6, 1, model_width)
    masked = span_mask(starts, lengths, seq_length)
    start_rows = jnp.where(
        masked[:, :, None],
        mask_embed.astype(jnp.float32),
        token_rows.astype(jnp.float32).reshape(seq_count, seq_length, model_width),
    )
    first_normed = modulate(
        start_rows, norm_first.astype(jnp.float32), modulation[:, 0], modulation[:, 1]
    ).astype(jnp.bfloat16)
    projected_rows = jnp.dot(
        first_normed.reshape(row_count, model_width),
        query_key_value_weight,
        preferred_element_type=jnp.float32,
    )
    projected_rows = projected_rows.reshape(seq_count, seq_length, 3, head_count, HEAD)
    cosine, sine_table = rotary_tables(seq_length, HEAD)
    queries = rotate(projected_rows[:, :, 0], cosine, sine_table).astype(jnp.bfloat16)
    keys_all = rotate(projected_rows[:, :, 1], cosine, sine_table).astype(jnp.bfloat16)
    values_all = projected_rows[:, :, 2].astype(jnp.bfloat16)
    mixed_values, log_totals = attend(queries, keys_all, values_all)
    attended_rows = jnp.dot(
        mixed_values.reshape(row_count, model_width),
        output_weight,
        preferred_element_type=jnp.float32,
    ).reshape(seq_count, seq_length, model_width)
    middle = start_rows + modulation[:, 2] * attended_rows
    second_normed = (
        modulate(middle, norm_second.astype(jnp.float32), modulation[:, 3], modulation[:, 4])
        .astype(jnp.bfloat16)
        .reshape(row_count, model_width)
    )
    upper_hidden = jnp.dot(
        second_normed, up_projection_weight, preferred_element_type=jnp.float32
    ) + up_projection_bias.astype(jnp.float32)
    active_units = gelu_tanh(upper_hidden).astype(jnp.bfloat16)
    branch_output = (
        jnp.dot(active_units, down_projection_weight, preferred_element_type=jnp.float32)
        + down_projection_bias.astype(jnp.float32)
    ).reshape(seq_count, seq_length, model_width)
    block_out = middle + modulation[:, 5] * branch_output
    stored = (
        features,
        modulation,
        masked,
        start_rows,
        first_normed,
        queries,
        keys_all,
        values_all,
        mixed_values,
        log_totals,
        attended_rows,
        middle,
        second_normed,
        upper_hidden,
        active_units,
        branch_output,
    )
    return (block_out.reshape(row_count, model_width).astype(jnp.bfloat16), stored)


def backward_pass(weights, stored, cot_rows):
    (
        mask_embed,
        ada_weight,
        ada_bias,
        norm_first,
        query_key_value_weight,
        output_weight,
        norm_second,
        up_projection_weight,
        up_projection_bias,
        down_projection_weight,
        down_projection_bias,
    ) = weights
    (
        features,
        modulation,
        masked,
        start_rows,
        first_normed,
        queries,
        keys_all,
        values_all,
        mixed_values,
        log_totals,
        attended_rows,
        middle,
        second_normed,
        upper_hidden,
        active_units,
        branch_output,
    ) = stored
    seq_count, seq_length, model_width = start_rows.shape
    row_count = seq_count * seq_length
    head_count = model_width // HEAD
    grad_out = cot_rows.astype(jnp.float32).reshape(seq_count, seq_length, model_width)
    d_gate_two = jnp.sum(grad_out * branch_output, axis=1, keepdims=True)
    d_branch = (modulation[:, 5] * grad_out).astype(jnp.bfloat16).reshape(row_count, model_width)
    grad_down_weight = contract_rows(active_units, d_branch)
    grad_down_bias = jnp.sum(d_branch.astype(jnp.float32), axis=0)
    d_active = times_transposed(d_branch, down_projection_weight)
    gelu_pull = jax.vjp(gelu_tanh, upper_hidden)[1]
    d_upper = gelu_pull(d_active)[0].astype(jnp.bfloat16)
    grad_up_weight = contract_rows(second_normed, d_upper)
    grad_up_bias = jnp.sum(d_upper.astype(jnp.float32), axis=0)
    d_normed_two = times_transposed(d_upper, up_projection_weight).reshape(
        seq_count, seq_length, model_width
    )
    pull_two = jax.vjp(
        modulate, middle, norm_second.astype(jnp.float32), modulation[:, 3], modulation[:, 4]
    )[1]
    d_hidden, grad_norm_second, d_shift_two, d_scale_two = pull_two(d_normed_two)
    d_middle = grad_out + d_hidden
    d_gate_one = jnp.sum(d_middle * attended_rows, axis=1, keepdims=True)
    d_attended = (modulation[:, 2] * d_middle).astype(jnp.bfloat16).reshape(row_count, model_width)
    grad_out_weight = contract_rows(mixed_values.reshape(row_count, model_width), d_attended)
    d_mixture = times_transposed(d_attended, output_weight).astype(jnp.bfloat16)
    d_mixture = d_mixture.reshape(seq_count, seq_length, head_count, HEAD)
    d_queries, d_keys, d_values = attend_back(queries, keys_all, values_all, d_mixture, log_totals)
    cosine, sine_table = rotary_tables(seq_length, HEAD)
    d_projected = jnp.stack(
        [
            rotate_back(d_queries, cosine, sine_table),
            rotate_back(d_keys, cosine, sine_table),
            d_values,
        ],
        axis=2,
    )
    d_projected = d_projected.astype(jnp.bfloat16).reshape(row_count, 3 * model_width)
    grad_qkv_weight = contract_rows(first_normed.reshape(row_count, model_width), d_projected)
    d_normed_one = times_transposed(d_projected, query_key_value_weight).reshape(
        seq_count, seq_length, model_width
    )
    pull_one = jax.vjp(
        modulate, start_rows, norm_first.astype(jnp.float32), modulation[:, 0], modulation[:, 1]
    )[1]
    d_hidden, grad_norm_first, d_shift_one, d_scale_one = pull_one(d_normed_one)
    d_start = d_middle + d_hidden
    chosen = masked[:, :, None]
    grad_tokens = jnp.where(chosen, 0.0, d_start).reshape(row_count, model_width)
    grad_mask_embed = jnp.sum(jnp.where(chosen, d_start, 0.0), axis=(0, 1))
    d_modulation = jnp.concatenate(
        [d_shift_one, d_scale_one, d_gate_one, d_shift_two, d_scale_two, d_gate_two], axis=1
    ).reshape(seq_count, 6 * model_width)
    grad_ada_weight = lax.dot_general(
        features, d_modulation, (((0,), (0,)), ((), ())), precision=FULL_PRECISION
    )
    grad_ada_bias = jnp.sum(d_modulation, axis=0)
    grads = (
        grad_mask_embed,
        grad_ada_weight,
        grad_ada_bias,
        grad_norm_first,
        grad_qkv_weight,
        grad_out_weight,
        grad_norm_second,
        grad_up_weight,
        grad_up_bias,
        grad_down_weight,
        grad_down_bias,
    )
    return (grad_tokens, grads)


def per_device(
    tokens,
    timestep,
    span_start,
    span_length,
    mask_embed,
    ada_weight,
    ada_bias,
    norm_first,
    query_key_value_weight,
    output_weight,
    norm_second,
    up_projection_weight,
    up_projection_bias,
    down_projection_weight,
    down_projection_bias,
    cotangent,
):
    per_seqs = timestep.shape[0] // MICRO
    per_rows = tokens.shape[0] // MICRO
    out_blocks = []
    grad_blocks = []
    totals = None
    for micro_step in range(MICRO):
        row_lower = micro_step * per_rows
        seq_lower = micro_step * per_seqs
        token_rows = tokens[row_lower : row_lower + per_rows]
        cot_rows = cotangent[row_lower : row_lower + per_rows]
        step_ids = timestep[seq_lower : seq_lower + per_seqs]
        starts = span_start[seq_lower : seq_lower + per_seqs]
        lengths = span_length[seq_lower : seq_lower + per_seqs]
        ahead_weights = (
            lax.all_gather(mask_embed, "narrow", axis=0, tiled=True),
            lax.all_gather(ada_weight, "narrow", axis=1, tiled=True),
            lax.all_gather(ada_bias, "narrow", axis=0, tiled=True),
            lax.all_gather(norm_first, "narrow", axis=0, tiled=True),
            lax.all_gather(query_key_value_weight, "narrow", axis=0, tiled=True),
            lax.all_gather(output_weight, "narrow", axis=0, tiled=True),
            lax.all_gather(norm_second, "narrow", axis=0, tiled=True),
            lax.all_gather(up_projection_weight, "narrow", axis=0, tiled=True),
            lax.all_gather(up_projection_bias, "narrow", axis=0, tiled=True),
            lax.all_gather(down_projection_weight, "narrow", axis=0, tiled=True),
            lax.all_gather(down_projection_bias, "narrow", axis=0, tiled=True),
        )
        result, stored = forward_pass(ahead_weights, token_rows, step_ids, starts, lengths)
        behind_weights = (
            lax.all_gather(mask_embed, "narrow", axis=0, tiled=True),
            lax.all_gather(ada_weight, "narrow", axis=1, tiled=True),
            lax.all_gather(ada_bias, "narrow", axis=0, tiled=True),
            lax.all_gather(norm_first, "narrow", axis=0, tiled=True),
            lax.all_gather(query_key_value_weight, "narrow", axis=0, tiled=True),
            lax.all_gather(output_weight, "narrow", axis=0, tiled=True),
            lax.all_gather(norm_second, "narrow", axis=0, tiled=True),
            lax.all_gather(up_projection_weight, "narrow", axis=0, tiled=True),
            lax.all_gather(up_projection_bias, "narrow", axis=0, tiled=True),
            lax.all_gather(down_projection_weight, "narrow", axis=0, tiled=True),
            lax.all_gather(down_projection_bias, "narrow", axis=0, tiled=True),
        )
        grad_rows, grads = backward_pass(behind_weights, stored, cot_rows)
        out_blocks.append(result)
        grad_blocks.append(grad_rows)
        shares = (
            lax.psum_scatter(grads[0], "narrow", scatter_dimension=0, tiled=True),
            lax.psum_scatter(grads[1], "narrow", scatter_dimension=1, tiled=True),
            lax.psum_scatter(grads[2], "narrow", scatter_dimension=0, tiled=True),
            lax.psum_scatter(grads[3], "narrow", scatter_dimension=0, tiled=True),
            lax.psum_scatter(grads[4], "narrow", scatter_dimension=0, tiled=True),
            lax.psum_scatter(grads[5], "narrow", scatter_dimension=0, tiled=True),
            lax.psum_scatter(grads[6], "narrow", scatter_dimension=0, tiled=True),
            lax.psum_scatter(grads[7], "narrow", scatter_dimension=0, tiled=True),
            lax.psum_scatter(grads[8], "narrow", scatter_dimension=0, tiled=True),
            lax.psum_scatter(grads[9], "narrow", scatter_dimension=0, tiled=True),
            lax.psum_scatter(grads[10], "narrow", scatter_dimension=0, tiled=True),
        )
        summed = lax.psum(
            (
                shares[0],
                shares[1],
                shares[2],
                shares[3],
                shares[4],
                shares[5],
                shares[6],
                shares[7],
                shares[8],
                shares[9],
                shares[10],
            ),
            "wide",
        )
        if totals is None:
            totals = tuple(summed)
        else:
            totals = tuple((running + update for running, update in zip(totals, summed)))
    return (
        jnp.concatenate(out_blocks, axis=0),
        jnp.concatenate(grad_blocks, axis=0),
        totals[0],
        totals[1],
        totals[2],
        totals[3],
        totals[4],
        totals[5],
        totals[6],
        totals[7],
        totals[8],
        totals[9],
        totals[10],
    )


def solution(mesh):
    return jax.shard_map(
        per_device,
        mesh=mesh,
        in_specs=(
            P(("wide", "narrow"), None),
            P(("wide", "narrow")),
            P(("wide", "narrow")),
            P(("wide", "narrow")),
            P("narrow"),
            P(None, "narrow"),
            P("narrow"),
            P("narrow"),
            P("narrow", None),
            P("narrow", None),
            P("narrow"),
            P("narrow", None),
            P("narrow"),
            P("narrow", None),
            P("narrow"),
            P(("wide", "narrow"), None),
        ),
        out_specs=(
            P(("wide", "narrow"), None),
            P(("wide", "narrow"), None),
            P("narrow"),
            P(None, "narrow"),
            P("narrow"),
            P("narrow"),
            P("narrow", None),
            P("narrow", None),
            P("narrow"),
            P("narrow", None),
            P("narrow"),
            P("narrow", None),
            P("narrow"),
        ),
        check_vma=False,
    )
```

profile of v0, /device:TPU:0, one launch (start us, length us, event | category | flops | bytes accessed | tf_op | source)
XLA Modules:
  0.0 1512.2 jit_solution(2210353919477805584)
XLA Ops:
  147.5 70.5 %while.94 = (s32[]{:T(128)}, bf16[2,512,12,64]{1,3,2,0:T(8,128)(2,1)}, f32[2,12,512]{2,1,0:T(8,128)S(1)}, bf16[2,512,12,64]{1,3,2,0:T(8,128)(2,1)}, bf16[1024,12...) while((s32[]{:T(128)}, bf16[2,512,12,64]{1,3,2,0:T(8,128)(2,1)}, ...), condition=%wide.region_5.6_spmd, body=%wide.region_2.5_spmd.sunk | while | flops 1667622912 | bytes 93036704 | solution.py:99
  219.9 70.4 %while.95 = (s32[]{:T(128)}, bf16[2,512,12,64]{1,3,2,0:T(8,128)(2,1)}, f32[2,12,512]{2,1,0:T(8,128)S(1)}, bf16[2,512,12,64]{1,3,2,0:T(8,128)(2,1)}, bf16[1024,12...) while((s32[]{:T(128)}, bf16[2,512,12,64]{1,3,2,0:T(8,128)(2,1)}, ...), condition=%wide.region_13.14_spmd, body=%wide.region_10.13_spmd.sunk | while | flops 1667622912 | bytes 93036704 | solution.py:99
  317.6 17.2 %multiply_convert_fusion.3 = (bf16[1024,3072]{1,0:T(8,128)(2,1)}, bf16[1024,3072]{1,0:T(8,128)(2,1)}, f32[1024,3072]{1,0:T(8,128)}) fusion(f32[3072]{0:T(1024)S(1)} %bitcast.338, f32[1024,3072]{1,0:T(8,128)} %fusion.142, bf16[768,3072]{1,0:T(8,128)(2,1)S(1)} %copy-done.159, f32[1024,768]{1,0:T(8,128)S(1)} %get-tuple-element.524, f32[768]{0:T(1024)S(1)} %copy-done.94, ...), kind=kOutput, calls=%fused_computation.101 | convolution fusion | flops 4899471360 | bytes 45642752 | tf_op jit(solution)/shard_map/dot_general | solution.py:214
  334.8 17.3 %convert_reduce_fusion.1 = (f32[3072]{0:T(1024)}, bf16[1024,3072]{1,0:T(8,128)(2,1)S(1)}) fusion(f32[1024,3072]{1,0:T(8,128)} %get-tuple-element.601, f32[3072]{0:T(1024)S(1)} %bitcast.339, bf16[3072,768]{1,0:T(8,128)(2,1)} %all-gather.16.cloned.1.call-done, f32[768]{0:T(1024)S(1)} %copy-done.142, bf16[2048,768]{1,0:T(8,128)(2,1)} %param.39), kind=kOutput, calls=%fused_computation.99 | convolution fusion | flops 4906546176 | bytes 25193472 | tf_op jit(solution)/shard_map/dot_general | solution.py:68
  360.2 17.1 %convert_reduce_fusion = (f32[3072]{0:T(1024)}, bf16[1024,3072]{1,0:T(8,128)(2,1)S(1)}) fusion(f32[1024,3072]{1,0:T(8,128)} %fusion.142, f32[3072]{0:T(1024)S(1)} %bitcast.340, bf16[3072,768]{1,0:T(8,128)(2,1)} %all-gather.16.cloned.1.call-done, f32[768]{0:T(1024)S(1)} %copy-done.144, bf16[2048,768]{1,0:T(8,128)(2,1)} %param.39), kind=kOutput, calls=%fused_computation.98 | convolution fusion | flops 4906546176 | bytes 25193472 | tf_op jit(solution)/shard_map/dot_general | solution.py:68
  427.5 225.2 %while.96 = (s32[]{:T(128)}, f32[1024,12,64]{0,2,1:T(8,128)}, f32[1024,12,64]{0,2,1:T(8,128)}, f32[2,512,12,64]{1,0,3,2:T(2,128)}, bf16[2,512,12,64]{1,3,2,0:T(8...) while((s32[]{:T(128)}, f32[1024,12,64]{0,2,1:T(8,128)}, ...), condition=%wide.region_20.21_spmd.clone, body=%wide.region_18.20_spmd.clone.sunk | while | flops 4106348544 | bytes 223518896 | solution.py:152
  451.8 16.8 %multiply_reduce_fusion.28 = (f32[12,512]{1,0:T(8,128)S(1)}, f32[12,512,1024]{2,1,0:T(8,128)}) fusion(f32[12,512,1024]{2,1,0:T(8,128)} %fusion.251, f32[12,512]{1,0:T(8,128)S(1)} %dynamic-slice_bitcast_fusion.4, bf16[1024,12,64]{0,2,1:T(8,128)(2,1)} %get-tuple-element.924, bf16[2,512,12,64]{1,3,2,0:T(8,128)(2,1)} %get-tuple-element.923, s32[]{:T(128)S(6)} %copy.176), kind=kOutput, calls=%fused_computation.29.clone.1 | convolution fusion | flops 830466048 | bytes 52740100 | tf_op jit(solution)/shard_map/while/body/eval_jaxpr/while/body/eval_jaxpr/qhd,khd->hqk/dot_general | solution.py:126
  468.7 21.5 %multiply_convert_fusion.12 = bf16[12,512,1024]{2,1,0:T(8,128)(2,1)} fusion(f32[12,512,1024]{2,1,0:T(8,128)} %get-tuple-element.806, f32[12,512,1024]{2,1,0:T(8,128)} %fusion.251, f32[12,512]{1,0:T(8,128)S(1)} %get-tuple-element.807, f32[12,512]{1,0:T(8,128)S(1)} %dynamic-slice_bitcast_fusion.4), kind=kLoop, calls=%fused_computation.28.clone.1 | loop fusion | flops 31457280 | bytes 62963712 | tf_op jit(solution)/shard_map/while/body/eval_jaxpr/while/body/eval_jaxpr/convert_element_type | solution.py:137
  510.3 28.8 %dynamic_update_slice.60 = f32[2,512,12,64]{1,0,3,2:T(2,128)} dynamic-update-slice(f32[2,512,12,64]{1,0,3,2:T(2,128)} %get-tuple-element.908, f32[1,512,12,64]{1,0,3,2:T(1,128)S(1)} %copy.130, s32[]{:T(128)S(6)} %copy.176, s32[]{:T(128)} %constant.184.clone.1..sunk, s32[]{:T(128)} %constant.184.clone.1..sunk, s32[]{:T(128)} %constant.184.clone.1..sunk) | dynamic-update-slice | bytes 3145732 | tf_op jit(solution)/shard_map/while/body/eval_jaxpr/while/body/jit(dynamic_update_index_in_dim)/dynamic_update_slice | solution.py:152
  564.2 16.8 %multiply_reduce_fusion.28 = (f32[12,512]{1,0:T(8,128)S(1)}, f32[12,512,1024]{2,1,0:T(8,128)}) fusion(f32[12,512,1024]{2,1,0:T(8,128)} %fusion.251, f32[12,512]{1,0:T(8,128)S(1)} %dynamic-slice_bitcast_fusion.4, bf16[1024,12,64]{0,2,1:T(8,128)(2,1)} %get-tuple-element.924, bf16[2,512,12,64]{1,3,2,0:T(8,128)(2,1)} %get-tuple-element.923, s32[]{:T(128)S(6)} %copy.176), kind=kOutput, calls=%fused_computation.29.clone.1 | convolution fusion | flops 830466048 | bytes 52740100 | tf_op jit(solution)/shard_map/while/body/eval_jaxpr/while/body/eval_jaxpr/qhd,khd->hqk/dot_general | solution.py:126
  581.0 21.5 %multiply_convert_fusion.12 = bf16[12,512,1024]{2,1,0:T(8,128)(2,1)} fusion(f32[12,512,1024]{2,1,0:T(8,128)} %get-tuple-element.806, f32[12,512,1024]{2,1,0:T(8,128)} %fusion.251, f32[12,512]{1,0:T(8,128)S(1)} %get-tuple-element.807, f32[12,512]{1,0:T(8,128)S(1)} %dynamic-slice_bitcast_fusion.4), kind=kLoop, calls=%fused_computation.28.clone.1 | loop fusion | flops 31457280 | bytes 62963712 | tf_op jit(solution)/shard_map/while/body/eval_jaxpr/while/body/eval_jaxpr/convert_element_type | solution.py:137
  623.5 28.8 %dynamic_update_slice.60 = f32[2,512,12,64]{1,0,3,2:T(2,128)} dynamic-update-slice(f32[2,512,12,64]{1,0,3,2:T(2,128)} %get-tuple-element.908, f32[1,512,12,64]{1,0,3,2:T(1,128)S(1)} %copy.130, s32[]{:T(128)S(6)} %copy.176, s32[]{:T(128)} %constant.184.clone.1..sunk, s32[]{:T(128)} %constant.184.clone.1..sunk, s32[]{:T(128)} %constant.184.clone.1..sunk) | dynamic-update-slice | bytes 3145732 | tf_op jit(solution)/shard_map/while/body/eval_jaxpr/while/body/jit(dynamic_update_index_in_dim)/dynamic_update_slice | solution.py:152
  674.7 224.9 %while.97 = (s32[]{:T(128)}, f32[1024,12,64]{0,2,1:T(8,128)}, f32[1024,12,64]{0,2,1:T(8,128)}, f32[2,512,12,64]{1,0,3,2:T(2,128)}, bf16[2,512,12,64]{1,3,2,0:T(8...) while((s32[]{:T(128)}, f32[1024,12,64]{0,2,1:T(8,128)}, ...), condition=%wide.region_27.28_spmd.clone, body=%wide.region_25.27_spmd.clone.sunk | while | flops 4106348544 | bytes 223518896 | solution.py:152
  698.8 16.8 %multiply_reduce_fusion.29 = (f32[12,512]{1,0:T(8,128)S(1)}, f32[12,512,1024]{2,1,0:T(8,128)}) fusion(f32[12,512,1024]{2,1,0:T(8,128)} %fusion.261, f32[12,512]{1,0:T(8,128)S(1)} %dynamic-slice_bitcast_fusion.5, bf16[1024,12,64]{0,2,1:T(8,128)(2,1)} %get-tuple-element.891, bf16[2,512,12,64]{1,3,2,0:T(8,128)(2,1)} %get-tuple-element.890, s32[]{:T(128)S(6)} %copy.164), kind=kOutput, calls=%fused_computation.55.clone.1 | convolution fusion | flops 830466048 | bytes 52740100 | tf_op jit(solution)/shard_map/while/body/eval_jaxpr/while/body/eval_jaxpr/qhd,khd->hqk/dot_general | solution.py:126
  715.6 21.5 %multiply_convert_fusion.13 = bf16[12,512,1024]{2,1,0:T(8,128)(2,1)} fusion(f32[12,512,1024]{2,1,0:T(8,128)} %get-tuple-element.817, f32[12,512,1024]{2,1,0:T(8,128)} %fusion.261, f32[12,512]{1,0:T(8,128)S(1)} %get-tuple-element.818, f32[12,512]{1,0:T(8,128)S(1)} %dynamic-slice_bitcast_fusion.5), kind=kLoop, calls=%fused_computation.54.clone.1 | loop fusion | flops 31457280 | bytes 62963712 | tf_op jit(solution)/shard_map/while/body/eval_jaxpr/while/body/eval_jaxpr/convert_element_type | solution.py:137
  757.4 28.8 %dynamic_update_slice.61 = f32[2,512,12,64]{1,0,3,2:T(2,128)} dynamic-update-slice(f32[2,512,12,64]{1,0,3,2:T(2,128)} %get-tuple-element.875, f32[1,512,12,64]{1,0,3,2:T(1,128)S(1)} %copy.131, s32[]{:T(128)S(6)} %copy.164, s32[]{:T(128)} %constant.184.clone.1..sunk.1, s32[]{:T(128)} %constant.184.clone.1..sunk.1, s32[]{:T(128)} %constant.184.clone.1..sunk.1) | dynamic-update-slice | bytes 3145732 | tf_op jit(solution)/shard_map/while/body/eval_jaxpr/while/body/jit(dynamic_update_index_in_dim)/dynamic_update_slice | solution.py:152
  811.1 16.8 %multiply_reduce_fusion.29 = (f32[12,512]{1,0:T(8,128)S(1)}, f32[12,512,1024]{2,1,0:T(8,128)}) fusion(f32[12,512,1024]{2,1,0:T(8,128)} %fusion.261, f32[12,512]{1,0:T(8,128)S(1)} %dynamic-slice_bitcast_fusion.5, bf16[1024,12,64]{0,2,1:T(8,128)(2,1)} %get-tuple-element.891, bf16[2,512,12,64]{1,3,2,0:T(8,128)(2,1)} %get-tuple-element.890, s32[]{:T(128)S(6)} %copy.164), kind=kOutput, calls=%fused_computation.55.clone.1 | convolution fusion | flops 830466048 | bytes 52740100 | tf_op jit(solution)/shard_map/while/body/eval_jaxpr/while/body/eval_jaxpr/qhd,khd->hqk/dot_general | solution.py:126
  828.0 21.5 %multiply_convert_fusion.13 = bf16[12,512,1024]{2,1,0:T(8,128)(2,1)} fusion(f32[12,512,1024]{2,1,0:T(8,128)} %get-tuple-element.817, f32[12,512,1024]{2,1,0:T(8,128)} %fusion.261, f32[12,512]{1,0:T(8,128)S(1)} %get-tuple-element.818, f32[12,512]{1,0:T(8,128)S(1)} %dynamic-slice_bitcast_fusion.5), kind=kLoop, calls=%fused_computation.54.clone.1 | loop fusion | flops 31457280 | bytes 62963712 | tf_op jit(solution)/shard_map/while/body/eval_jaxpr/while/body/eval_jaxpr/convert_element_type | solution.py:137
  870.7 28.8 %dynamic_update_slice.61 = f32[2,512,12,64]{1,0,3,2:T(2,128)} dynamic-update-slice(f32[2,512,12,64]{1,0,3,2:T(2,128)} %get-tuple-element.875, f32[1,512,12,64]{1,0,3,2:T(1,128)S(1)} %copy.131, s32[]{:T(128)S(6)} %copy.164, s32[]{:T(128)} %constant.184.clone.1..sunk.1, s32[]{:T(128)} %constant.184.clone.1..sunk.1, s32[]{:T(128)} %constant.184.clone.1..sunk.1) | dynamic-update-slice | bytes 3145732 | tf_op jit(solution)/shard_map/while/body/eval_jaxpr/while/body/jit(dynamic_update_index_in_dim)/dynamic_update_slice | solution.py:152
  1035.8 39.6 %reduce-scatter.8.cloned.1.call-done = f32[192,2304]{1,0:T(8,128)} async-done(((f32[768,2304]{1,0:T(8,128)}), f32[192,2304]{1,0:T(8,128)}) %reduce-scatter.8.cloned.1.call-update) | async-done | bytes 1769488 | tf_op jit(solution)/shard_map/reduce_scatter | solution.py:414
  1075.4 81.3 %reduce-scatter.14.cloned.1.call-done = f32[768,768]{1,0:T(8,128)} async-done(((f32[3072,768]{1,0:T(8,128)}), f32[768,768]{1,0:T(8,128)}) %reduce-scatter.14.cloned.1.call-update) | async-done | bytes 2359312 | tf_op jit(solution)/shard_map/reduce_scatter | solution.py:419
  1156.7 81.1 %reduce-scatter.12.cloned.1.call-done = f32[192,3072]{1,0:T(8,128)} async-done(((f32[768,3072]{1,0:T(8,128)}), f32[192,3072]{1,0:T(8,128)}) %reduce-scatter.12.cloned.1.call-update) | async-done | bytes 2359312 | tf_op jit(solution)/shard_map/reduce_scatter | solution.py:417
  1251.3 40.1 %all-reduce.10 = (f32[192]{0:T(256)}, f32[1152]{0:T(1024)}, f32[192]{0:T(256)}, f32[192]{0:T(256)}, f32[768]{0:T(1024)}, /*index=5*/f32[192]{0:T(256)}) all-reduce(f32[192]{0:T(256)S(1)} %dynamic-slice.7, f32[1152]{0:T(1024)S(1)} %dynamic-slice.9, f32[192]{0:T(256)S(1)} %dynamic-slice.11, ...), channel_id=1, replica_groups=mesh['wide'=8,'narrow'=4] {'wide'}, use_global_device_ids=true, to_apply=%region_32.33 | all-reduce | flops 2688 | bytes 21504 | tf_op jit(solution)/shard_map/psum | solution.py:422
  1298.6 198.4 %all-reduce.16.cloned.1.call-done = (f32[128,1152]{1,0:T(8,128)}, f32[192,2304]{1,0:T(8,128)}, f32[192,768]{1,0:T(8,128)}, f32[192,3072]{1,0:T(8,128)}, f32[768,768]{1,0:T(8,128)}) async-done(((f32[128,1152]{1,0:T(8,128)}, f32[192,2304]{1,0:T(8,128)}, f32[192,768]{1,0:T(8,128)}, f32[192,3072]{1,0:T(8,128)}, f32[768,768]{1,0:T(8,128)}), (f32[128,1152]{1,0:T(8,128)}, f32[192,2304]{1,0:T(8,128)}, ...) | async-done | bytes 7667728 | tf_op jit(solution)/shard_map/psum | solution.py:422
  (595 shorter events, 727.1 us)
Async XLA Ops:
  7.3 39.1 %all-gather.8.cloned.1.call-start = ((), (), s32[]{:S(2)}) async-start(), calls=%async_computation.5 | async-start | bytes 1474560 | tf_op jit(solution)/shard_map/all_gather | solution.py:381
  8.0 54.5 %all-gather.10.cloned.1.call-start = ((), (), s32[]{:S(2)}) async-start(), calls=%async_computation.6 | async-start | bytes 4423680 | tf_op jit(solution)/shard_map/all_gather | solution.py:384
  8.8 288.4 %all-gather.12.cloned.1.call-start = ((), (), s32[]{:S(2)}) async-start(), calls=%async_computation.7 | async-start | bytes 1474560 | tf_op jit(solution)/shard_map/all_gather | solution.py:385
  9.5 296.3 %all-gather.14.cloned.1.call-start = ((), (), s32[]{:S(2)}) async-start(), calls=%async_computation.8 | async-start | bytes 5898240 | tf_op jit(solution)/shard_map/all_gather | solution.py:387
  10.1 324.7 %all-gather.16.cloned.1.call-start = ((), (), s32[]{:S(2)}) async-start(), calls=%async_computation.9 | async-start | bytes 5898240 | tf_op jit(solution)/shard_map/all_gather | solution.py:389
  10.7 1025.1 %reduce-scatter.10.cloned.1.call-start = ((), (), s32[]{:S(2)}) async-start(), calls=%async_computation.12 | async-start | bytes 2949120 | tf_op jit(solution)/shard_map/reduce_scatter | solution.py:415
  23.6 58.3 %copy-start.91 = (f32[768]{0:T(1024)}, f32[768]{0:T(1024)S(1)}, u32[]{:S(2)}) copy-start(f32[768]{0:T(1024)S(1)} %convert_element_type.206) | copy-start | bytes 9220
  24.2 57.7 %copy-start.115 = (f32[768]{0:T(1024)}, f32[768]{0:T(1024)S(1)}, u32[]{:S(2)}) copy-start(f32[768]{0:T(1024)S(1)} %convert_element_type.210) | copy-start | bytes 9220
  29.9 52.0 %copy-start.112 = (pred[1024]{0:T(1024)(128)(4,1)}, pred[1024]{0:T(1024)(128)(4,1)S(1)}, u32[]{:S(2)}) copy-start(pred[1024]{0:T(1024)(128)(4,1)S(1)} %fusion.123) | copy-start | bytes 3076
  31.3 50.6 %copy-start.100 = (f32[1024]{0:T(1024)}, f32[1024]{0:T(1024)S(1)}, u32[]{:S(2)}) copy-start(f32[1024]{0:T(1024)S(1)} %broadcast_multiply_fusion.3) | copy-start | bytes 12292
  45.6 87.5 %copy-start.55 = (f32[1024,64]{0,1:T(8,128)}, f32[1024,64]{0,1:T(8,128)S(1)}, u32[]{:S(2)}) copy-start(f32[1024,64]{0,1:T(8,128)S(1)} %get-tuple-element.617) | copy-start | bytes 786436
  147.5 72.4 %copy-start = (bf16[1024,12,64]{0,2,1:T(8,128)(2,1)S(1)}, bf16[1024,12,64]{0,2,1:T(8,128)(2,1)}, u32[]{:S(2)}) copy-start(bf16[1024,12,64]{0,2,1:T(8,128)(2,1)} %get-tuple-element.866) | copy-start | bytes 4718596
  304.1 96.5 %copy-start.11 = (f32[1024,768]{1,0:T(8,128)}, f32[1024,768]{1,0:T(8,128)S(1)}, u32[]{:S(2)}) copy-start(f32[1024,768]{1,0:T(8,128)S(1)} %get-tuple-element.524) | copy-start | bytes 9437188
  304.2 73.1 %copy-start.81 = (f32[1024]{0:T(1024)}, f32[1024]{0:T(1024)S(1)}, u32[]{:S(2)}) copy-start(f32[1024]{0:T(1024)S(1)} %broadcast_multiply_fusion.4) | copy-start | bytes 12292
  304.2 96.4 %copy-start.79 = (f32[1024]{0:T(1024)}, f32[1024]{0:T(1024)S(1)}, u32[]{:S(2)}) copy-start(f32[1024]{0:T(1024)S(1)} %broadcast_multiply_fusion.2) | copy-start | bytes 12292
  304.8 95.9 %copy-start.83 = (f32[1024]{0:T(1024)}, f32[1024]{0:T(1024)S(1)}, u32[]{:S(2)}) copy-start(f32[1024]{0:T(1024)S(1)} %fusion.127) | copy-start | bytes 12292
  305.9 71.4 %copy-start.85 = (f32[1024]{0:T(1024)}, f32[1024]{0:T(1024)S(1)}, u32[]{:S(2)}) copy-start(f32[1024]{0:T(1024)S(1)} %fusion.125) | copy-start | bytes 12292
  915.3 120.6 %reduce-scatter.6.cloned.1.call-start = ((), (), s32[]{:S(2)}) async-start(), calls=%async_computation.10 | async-start | bytes 2949120 | tf_op jit(solution)/shard_map/reduce_scatter | solution.py:411
  976.0 99.5 %reduce-scatter.8.cloned.1.call-start = ((), (), s32[]{:S(2)}) async-start(), calls=%async_computation.11 | async-start | bytes 8847360 | tf_op jit(solution)/shard_map/reduce_scatter | solution.py:414
  993.6 163.2 %reduce-scatter.14.cloned.1.call-start = ((), (), s32[]{:S(2)}) async-start(), calls=%async_computation.14 | async-start | bytes 11796480 | tf_op jit(solution)/shard_map/reduce_scatter | solution.py:419
  1013.5 224.3 %reduce-scatter.12.cloned.1.call-start = ((), (), s32[]{:S(2)}) async-start(), calls=%async_computation.13 | async-start | bytes 11796480 | tf_op jit(solution)/shard_map/reduce_scatter | solution.py:417
  1035.7 461.2 %all-reduce.16.cloned.1.call-start = ((), (), s32[]{:S(2)}) async-start(), calls=%async_computation.15 | async-start | bytes 15335424 | tf_op jit(solution)/shard_map/psum | solution.py:422
  1237.8 53.6 %copy-start.64 = (bf16[1024,768]{1,0:T(8,128)(2,1)S(1)}, bf16[1024,768]{1,0:T(8,128)(2,1)}, u32[]{:S(2)}) copy-start(bf16[1024,768]{1,0:T(8,128)(2,1)} %get-tuple-element.543) | copy-start | bytes 4718596
  1237.9 53.6 %copy-start.65 = (bf16[1024,768]{1,0:T(8,128)(2,1)S(1)}, bf16[1024,768]{1,0:T(8,128)(2,1)}, u32[]{:S(2)}) copy-start(bf16[1024,768]{1,0:T(8,128)(2,1)} %get-tuple-element.544) | copy-start | bytes 4718596
  (159 other events, 1143.3 us)
Sparse Core Ops, SparseCore 0:
  9.7 20.2 all-gather.7
  31.5 30.9 all-gather.9
  64.1 17.4 all-gather.11
  83.0 37.4 all-gather.13
  121.9 37.4 all-gather.15
  915.4 33.0 reduce-scatter.9
  976.1 33.0 reduce-scatter.5
  1011.7 63.6 reduce-scatter.7
  1078.2 78.4 reduce-scatter.13
  1159.3 78.4 reduce-scatter.11
  1243.6 253.3 all-reduce.15
where the time goes:
time: 1530 us; the launch traced here: 1510 us
  matrix products  543 us (35%)
  waiting for transfers between devices  415 us (27%)
  local copies, waits for them, and re-layouts  250 us (16%)
  other arithmetic  210 us (14%)
  blocking collectives  69.6 us (5%)
  between operations  23 us (2%)
    psum x1, waiting for transfers between devices, per_device(): lax.psum((shares[0], shares[1], shares[2], shares[3], shares[4], shares[5...  198 us
    dynamic_update_slice x8, local copies, waits for them, and re-layouts, per_sequence(): lax.scan(per_block, (zeros_init, zeros_init), (query_blocks, grad_blocks,...  122 us
    dot_general x8, matrix products, per_block(): jnp.einsum('qhd,khd->hqk', query_block, keys_seq, preferred_element_type=...  91 us
    convert_element_type x4, other arithmetic, per_block(): d_scores = (probs * (d_probs - jnp.sum(d_probs * probs, axis=-1, keepdims...  86 us
    reduce_scatter x1, waiting for transfers between devices, per_device(): lax.psum_scatter(grads[9], 'narrow', scatter_dimension=0, tiled=True)  81.3 us
    reduce_scatter x1, waiting for transfers between devices, per_device(): lax.psum_scatter(grads[7], 'narrow', scatter_dimension=0, tiled=True)  81.1 us
    dot_general x8, matrix products, times_transposed(): lax.dot_general(leading, trailing, (((1,), (1,)), ((), ())), preferred_el...  69.8 us
    dot_general x4, matrix products, per_block(): jnp.einsum('qhd,khd->hqk', grad_block, values_seq, preferred_element_type...  67.3 us
  transfers between devices with their start and end apart: 11, of which 5 were waited for; matrix products, arithmetic and copies ran while one was open for 26% of the time, Pallas kernels for 0%

commit v1 on v0

v1 whole, which is shorter than its diff:
```python
import math

import jax
import jax.numpy as jnp
from jax import lax
from jax.experimental import pallas as pl
from jax.experimental.pallas import tpu as pltpu
from jax.sharding import PartitionSpec as P

HEAD = 64
PAIR = 2 * HEAD
GROUPS = 3
EPSILON = 1e-05
FULL_PRECISION = lax.Precision.HIGHEST
F32 = jnp.float32
BF16 = jnp.bfloat16
SCALE = 1.0 / math.sqrt(HEAD)
SCALE2 = SCALE * math.log2(math.e)
VMEM_BYTES = 60 << 20
PLAIN = (((1,), (0,)), ((), ()))
TRANSPOSED = (((1,), (1,)), ((), ()))


def mxu(left, right, dims=PLAIN):
    return lax.dot_general(left, right, dims, preferred_element_type=F32)


def call(kernel, name, grid, in_specs, out_specs, out_shape, scratch, flops, moved, exps=0):
    return pl.pallas_call(
        kernel,
        name=name,
        grid=grid,
        in_specs=in_specs,
        out_specs=out_specs,
        out_shape=out_shape,
        scratch_shapes=scratch,
        compiler_params=pltpu.CompilerParams(vmem_limit_bytes=VMEM_BYTES),
        cost_estimate=pl.CostEstimate(flops=flops, bytes_accessed=moved, transcendentals=exps),
    )


def whole(shape):
    return pl.BlockSpec(shape, lambda *_: (0,) * len(shape), pipeline_mode=pl.Buffered(1))


def smem():
    return pl.BlockSpec(memory_space=pltpu.SMEM)


def time_features(step_ids, feature_count):
    halfway = feature_count // 2
    spacing = jnp.exp(-math.log(10000.0) * jnp.arange(halfway, dtype=F32) / halfway)
    angles = step_ids.astype(F32)[:, None] * spacing[None, :]
    return jax.nn.silu(jnp.concatenate([jnp.cos(angles), jnp.sin(angles)], axis=-1))


def rotary_tables(seq_length):
    halfway = HEAD // 2
    spacing = jnp.exp(-math.log(10000.0) * jnp.arange(halfway, dtype=F32) / halfway)
    angles = jnp.arange(seq_length, dtype=F32)[:, None] * spacing[None, :]
    cosine, sine = jnp.cos(angles), jnp.sin(angles)
    nothing = jnp.zeros_like(sine)
    cosines = jnp.concatenate([cosine] * 4, axis=-1)
    upper = jnp.concatenate([-sine, nothing] * 2, axis=-1)
    lower = jnp.concatenate([nothing, sine] * 2, axis=-1)
    return cosines, upper, lower


def from_ahead(v):
    return pltpu.roll(v, PAIR - HEAD // 2, 1)


def from_behind(v):
    return pltpu.roll(v, HEAD // 2, 1)


def masked_rows(tokens, embed, start, length, first_row):
    rows = tokens.shape[0]
    position = lax.broadcasted_iota(jnp.int32, (rows, 1), 0) + first_row
    inside = (position >= start) & (position < start + length)
    return jnp.where(inside, embed, tokens.astype(F32)), inside


def normalized(rows):
    centre = rows - jnp.mean(rows, axis=-1, keepdims=True)
    spread = jnp.mean(centre * centre, axis=-1, keepdims=True)
    inverse = lax.rsqrt(spread + EPSILON)
    return centre * inverse, inverse


def norm_back(d_out, hat, inverse):
    return inverse * (
        d_out
        - jnp.mean(d_out, axis=-1, keepdims=True)
        - hat * jnp.mean(d_out * hat, axis=-1, keepdims=True)
    )


def column_sum(v):
    return jnp.sum(v, axis=0, keepdims=True)


def project(tokens, span, embed, gain, modulation, weight, tables, seqs, block=512):
    rows, width = tokens.shape
    seq_length = rows // seqs
    block = min(block, seq_length)
    per_seq = seq_length // block
    pairs = width // PAIR

    def kernel(span_ref, tok, emb, gn, mod, w, cos, upp, low, out, nt):
        step = pl.program_id(0)
        seq = step // per_seq
        first = (step - seq * per_seq) * block
        start, _ = masked_rows(tok[...], emb[...], span_ref[0, seq], span_ref[1, seq], first)
        hat, _ = normalized(start)
        shift = mod[pl.ds(seq, 1), 0:width]
        scale = mod[pl.ds(seq, 1), width : 2 * width]
        normed = (hat * (gn[...] * (1.0 + scale)) + shift).astype(BF16)
        nt[...] = jnp.transpose(normed)
        acc = mxu(normed, w[...])
        for part in range(2 * pairs):
            v = acc[:, part * PAIR : (part + 1) * PAIR]
            v = v * cos[...] + from_ahead(v) * upp[...] + from_behind(v) * low[...]
            out[:, part * PAIR : (part + 1) * PAIR] = v.astype(BF16)
        out[:, 2 * width :] = acc[:, 2 * width :].astype(BF16)

    table = pl.BlockSpec((block, PAIR), lambda i: (lax.rem(i, per_seq), 0))
    return call(
        kernel,
        "project",
        (rows // block,),
        [
            smem(),
            pl.BlockSpec((block, width), lambda i: (i, 0)),
            whole((1, width)),
            whole((1, width)),
            whole(modulation.shape),
            whole(weight.shape),
            table,
            table,
            table,
        ],
        (
            pl.BlockSpec((block, 3 * width), lambda i: (i, 0)),
            pl.BlockSpec((width, block), lambda i: (0, i)),
        ),
        (
            jax.ShapeDtypeStruct((rows, 3 * width), BF16),
            jax.ShapeDtypeStruct((width, rows), BF16),
        ),
        [],
        2 * rows * width * 3 * width,
        rows * width * 10 + 6 * width * width,
    )(span, tokens, embed, gain, modulation, weight, *tables)


def head_mask(v, half):
    lane = lax.broadcasted_iota(jnp.int32, (1, PAIR), 1)
    keep = (lane < HEAD) if half == 0 else (lane >= HEAD)
    return jnp.where(keep, v, jnp.zeros_like(v))


def attend(qkv, seqs, block=512, per=3):
    rows, width = qkv.shape[0], qkv.shape[1] // 3
    seq_length = rows // seqs
    block = min(block, seq_length)
    pairs = width // PAIR
    count = seq_length // block
    steps = pairs // per
    items = per * count
    wide = per * PAIR

    def kernel(q_ref, k_ref, v_ref, out, total, v_turned, out_turned, held):
        v_turned[...] = jnp.transpose(v_ref[...])

        def place(i):
            pair = i // count
            part = i - pair * count
            return (
                pair,
                pl.ds(pl.multiple_of(pair * PAIR, PAIR), PAIR),
                pl.ds(pl.multiple_of(part * block, block), block),
            )

        def score(i, half):
            _, cols, part = place(i)
            held[half] = mxu(k_ref[:, cols], head_mask(q_ref[part, cols], half), TRANSPOSED)

        def finish(i, half):
            pair, _, part = place(i)
            scores = held[half]
            top = jnp.max(scores, axis=0, keepdims=True)
            exponent = jnp.exp2(scores * SCALE2 - top * SCALE2).astype(BF16)
            head = pl.ds(pl.multiple_of(pair * PAIR + half * HEAD, HEAD), HEAD)
            left = jnp.concatenate([v_turned[head, :], jnp.ones((16, seq_length), BF16)], axis=0)
            mixed = mxu(left, exponent)
            denominator = mixed[HEAD : HEAD + 1]
            out_turned[head, part] = mixed[:HEAD] * (1.0 / denominator)
            total[0, pair, half : half + 1, part] = top * SCALE2 + jnp.log2(denominator)

        score(0, 0)

        def body(i, carry):
            score(i, 1)
            finish(i, 0)
            score(jnp.minimum(i + 1, items - 1), 0)
            finish(i, 1)
            return carry

        lax.fori_loop(0, items, body, 0)
        out[...] = jnp.transpose(out_turned[...]).astype(BF16)

    def part_of(which):
        return pl.BlockSpec((seq_length, wide), lambda s, p: (s, which * steps + p))

    return call(
        kernel,
        "attend",
        (seqs, steps),
        [part_of(0), part_of(1), part_of(2)],
        (part_of(0), pl.BlockSpec((1, per, 2, seq_length), lambda s, p: (s, p, 0, 0))),
        (
            jax.ShapeDtypeStruct((rows, width), BF16),
            jax.ShapeDtypeStruct((seqs, pairs, 2, seq_length), F32),
        ),
        [
            pltpu.VMEM((wide, seq_length), BF16),
            pltpu.VMEM((wide, seq_length), F32),
            pltpu.VMEM((2, seq_length, block), F32),
        ],
        16 * rows * seq_length * width,
        rows * width * 8,
        rows * seq_length * width // HEAD,
    )(qkv, qkv, qkv)


def attend_back(qkv, mixture, d_mixture, total, tables, seqs, block=512, per=3):
    rows, width = mixture.shape
    seq_length = rows // seqs
    block = min(block, seq_length)
    pairs = width // PAIR
    count = seq_length // block
    steps = pairs // per
    items = per * count
    wide = per * PAIR

    def kernel(
        q_ref, k_ref, v_ref, mix, grad, tot, cos, upp, low, dq, dk, dv,
        k_turned, dq_turned, dk_sum, dv_sum, inner, s_held, p_held,
    ):
        k_turned[...] = jnp.transpose(k_ref[...])
        product = jnp.transpose(mix[...].astype(F32) * grad[...].astype(F32))
        for pair in range(per):
            for half in range(2):
                lower = pair * PAIR + half * HEAD
                inner[pair, half : half + 1, :] = column_sum(product[lower : lower + HEAD, :])
        dk_sum[...] = jnp.zeros_like(dk_sum)
        dv_sum[...] = jnp.zeros_like(dv_sum)

        def body(i, carry):
            pair = i // count
            part = i - pair * count
            cols = pl.ds(pl.multiple_of(pair * PAIR, PAIR), PAIR)
            part = pl.ds(pl.multiple_of(part * block, block), block)
            for half in range(2):
                head = pl.ds(pl.multiple_of(pair * PAIR + half * HEAD, HEAD), HEAD)
                query = head_mask(q_ref[part, cols], half)
                cot = head_mask(grad[part, cols], half)
                s_held[half] = mxu(k_ref[:, cols], query, TRANSPOSED)
                p_held[half] = mxu(v_ref[:, cols], cot, TRANSPOSED)
                probs = jnp.exp2(s_held[half] * SCALE2 - tot[0, pair, half : half + 1, part])
                d_scores = (probs * (p_held[half] - inner[pair, half : half + 1, part])).astype(BF16)
                dv_sum[:, cols] += mxu(probs.astype(BF16), cot)
                dk_sum[:, cols] += mxu(d_scores, query)
                dq_turned[head, part] = mxu(k_turned[head, :], d_scores)
            return carry

        lax.fori_loop(0, items, body, 0)
        d_queries = jnp.transpose(dq_turned[...])
        for source, target in ((d_queries, dq), (dk_sum, dk)):
            for pair in range(per):
                v = source[:, pair * PAIR : (pair + 1) * PAIR] * SCALE
                v = v * cos[...] - from_ahead(v) * upp[...] - from_behind(v) * low[...]
                target[:, pair * PAIR : (pair + 1) * PAIR] = v.astype(BF16)
        dv[...] = dv_sum[...].astype(BF16)

    def part_of(which):
        return pl.BlockSpec((seq_length, wide), lambda s, p: (s, which * steps + p))

    table = whole((seq_length, PAIR))
    grads = jax.ShapeDtypeStruct((rows, width), BF16)
    return call(
        kernel,
        "attend_back",
        (seqs, steps),
        [part_of(0), part_of(1), part_of(2), part_of(0), part_of(0)]
        + [pl.BlockSpec((1, per, 2, seq_length), lambda s, p: (s, p, 0, 0))]
        + [table] * 3,
        (part_of(0), part_of(0), part_of(0)),
        (grads, grads, grads),
        [
            pltpu.VMEM((wide, seq_length), BF16),
            pltpu.VMEM((wide, seq_length), F32),
            pltpu.VMEM((seq_length, wide), F32),
            pltpu.VMEM((seq_length, wide), F32),
            pltpu.VMEM((per, 2, seq_length), F32),
            pltpu.VMEM((2, seq_length, block), F32),
            pltpu.VMEM((2, seq_length, block), F32),
        ],
        40 * rows * seq_length * width,
        rows * width * 16,
        rows * seq_length * width // HEAD,
    )(qkv, qkv, qkv, mixture, d_mixture, total, *tables)


def middle_norm(mixture, tokens, span, embed, gain, modulation, weight, seqs, block=512):
    rows, width = tokens.shape
    seq_length = rows // seqs
    block = min(block, seq_length)
    per_seq = seq_length // block

    def kernel(span_ref, mix, tok, emb, gn, mod, w, out):
        step = pl.program_id(0)
        seq = step // per_seq
        first = (step - seq * per_seq) * block
        start, _ = masked_rows(tok[...], emb[...], span_ref[0, seq], span_ref[1, seq], first)
        middle = start + mod[pl.ds(seq, 1), 2 * width : 3 * width] * mxu(mix[...], w[...])
        hat, _ = normalized(middle)
        shift = mod[pl.ds(seq, 1), 3 * width : 4 * width]
        scale = mod[pl.ds(seq, 1), 4 * width : 5 * width]
        out[...] = (hat * (gn[...] * (1.0 + scale)) + shift).astype(BF16)

    row = pl.BlockSpec((block, width), lambda i: (i, 0))
    return call(
        kernel,
        "middle_norm",
        (rows // block,),
        [smem(), row, row, whole((1, width)), whole((1, width)), whole(modulation.shape)]
        + [whole(weight.shape)],
        row,
        jax.ShapeDtypeStruct((rows, width), BF16),
        [],
        2 * rows * width * width,
        rows * width * 6,
    )(span, mixture, tokens, embed, gain, modulation, weight)


def gelu_pair(v):
    root = math.sqrt(2.0 / math.pi)
    square = v * v
    bent = jnp.tanh(v * (root + (root * 0.044715) * square))
    near = 0.5 + 0.5 * bent
    slope = near + (0.5 * v) * (1.0 - bent * bent) * (root + (3.0 * root * 0.044715) * square)
    return v * near, slope


def hidden_units(normed, cot, modulation, up, up_bias, down, seqs, block=512, tile=256):
    rows, width = normed.shape
    units = up.shape[1]
    seq_length = rows // seqs
    block = min(block, seq_length)
    per_seq = seq_length // block
    steps = rows // block
    tiles = width // tile

    def kernel(nrm, g, mod, w_up, b_up, w_down, act, d_up, g_up, g_down, g_bias, b_down,
               n_turned, d_turned, a_held, u_held):
        step = pl.program_id(0)

        @pl.when(step == 0)
        def _():
            g_bias[...] = jnp.zeros_like(g_bias)
            b_down[...] = jnp.zeros_like(b_down)

        @pl.when(step < steps)
        def _():
            seq = step // per_seq
            part = pl.ds(pl.multiple_of(step * block, block), block)
            d_branch = (mod[pl.ds(seq, 1), 5 * width : 6 * width] * g[...].astype(F32)).astype(BF16)
            upper = mxu(nrm[...], w_up[...]) + b_up[...]
            active, slope = gelu_pair(upper)
            active = active.astype(BF16)
            d_upper = (mxu(d_branch, w_down[...], TRANSPOSED) * slope).astype(BF16)
            act[...] = active
            a_held[part, :] = active
            d_up[...] = d_upper
            u_held[part, :] = d_upper
            n_turned[:, part] = jnp.transpose(nrm[...])
            d_turned[:, part] = jnp.transpose(d_branch)
            g_bias[...] += column_sum(d_upper.astype(F32))
            b_down[...] += column_sum(d_branch.astype(F32))

        @pl.when(step >= steps)
        def _():
            part = pl.ds(pl.multiple_of((step - steps) * tile, tile), tile)
            g_up[...] = mxu(n_turned[part, :], u_held[...]).astype(BF16)
            g_down[...] = jnp.transpose(mxu(d_turned[part, :], a_held[...])).astype(BF16)

    def early(i):
        return (jnp.minimum(i, steps - 1), 0)

    def late(i):
        return jnp.maximum(i - steps, 0)

    return call(
        kernel,
        "hidden_units",
        (steps + tiles,),
        [
            pl.BlockSpec((block, width), early),
            pl.BlockSpec((block, width), early),
            whole(modulation.shape),
            whole(up.shape),
            whole(up_bias.shape),
            whole(down.shape),
        ],
        (
            pl.BlockSpec((block, units), early),
            pl.BlockSpec((block, units), early),
            pl.BlockSpec((tile, units), lambda i: (late(i), 0)),
            pl.BlockSpec((units, tile), lambda i: (0, late(i))),
            pl.BlockSpec((1, units), lambda i: (0, 0)),
            pl.BlockSpec((1, width), lambda i: (0, 0)),
        ),
        (
            jax.ShapeDtypeStruct((rows, units), BF16),
            jax.ShapeDtypeStruct((rows, units), BF16),
            jax.ShapeDtypeStruct((width, units), BF16),
            jax.ShapeDtypeStruct((units, width), BF16),
            jax.ShapeDtypeStruct((1, units), F32),
            jax.ShapeDtypeStruct((1, width), F32),
        ),
        [
            pltpu.VMEM((width, rows), BF16),
            pltpu.VMEM((width, rows), BF16),
            pltpu.VMEM((rows, units), BF16),
            pltpu.VMEM((rows, units), BF16),
        ],
        8 * rows * width * units,
        rows * (width * 4 + units * 4) + 8 * width * units,
        rows * units,
    )(normed, cot, modulation, up, up_bias, down)


def finish_block(
    mixture, tokens, cot, span, embed, gain, modulation, out_weight, down_bias,
    actives, d_uppers, ups, downs, seqs, block=256,
):
    rows, width = tokens.shape
    seq_length = rows // seqs
    block = min(block, seq_length)
    per_seq = seq_length // block
    groups = len(actives)
    units = actives[0].shape[1]

    def kernel(*refs):
        span_ref, mix, tok, g, emb, gn, mod, w_out, b_down = refs[:9]
        acts, d_ups = refs[9 : 9 + groups], refs[9 + groups : 9 + 2 * groups]
        w_ups = refs[9 + 2 * groups : 9 + 3 * groups]
        w_downs = refs[9 + 3 * groups : 9 + 4 * groups]
        block_out, d_middle_out, d_mix, g_out, sums, g_sum = refs[9 + 4 * groups :]
        step = pl.program_id(0)
        seq = step // per_seq
        first = (step - seq * per_seq) * block

        @pl.when(step == 0)
        def _():
            g_sum[...] = jnp.zeros_like(g_sum)

        @pl.when(step == seq * per_seq)
        def _():
            sums[...] = jnp.zeros_like(sums)

        def vector(which):
            return mod[pl.ds(seq, 1), which * width : (which + 1) * width]

        cotangent = g[...].astype(F32)
        attended = mxu(mix[...], w_out[...])
        start, _ = masked_rows(tok[...], emb[...], span_ref[0, seq], span_ref[1, seq], first)
        middle = start + vector(2) * attended
        hat, inverse = normalized(middle)
        branch = mxu(acts[0][...], w_downs[0][...])
        for group in range(1, groups):
            branch += mxu(acts[group][...], w_downs[group][...])
        branch += b_down[...]
        block_out[...] = (middle + vector(5) * branch).astype(BF16)
        d_normed = mxu(d_ups[0][...], w_ups[0][...], TRANSPOSED)
        for group in range(1, groups):
            d_normed += mxu(d_ups[group][...], w_ups[group][...], TRANSPOSED)
        d_middle = cotangent + norm_back(d_normed * (gn[...] * (1.0 + vector(4))), hat, inverse)
        d_middle_out[...] = d_middle
        d_attended = (vector(2) * d_middle).astype(BF16)
        d_mix[...] = mxu(d_attended, w_out[...], TRANSPOSED).astype(BF16)
        g_sum[...] += mxu(jnp.transpose(mix[...]), d_attended)
        sums[0, 0:1, :] += column_sum(cotangent * branch)
        sums[0, 1:2, :] += column_sum(d_normed)
        sums[0, 2:3, :] += column_sum(d_normed * hat)
        sums[0, 3:4, :] += column_sum(d_middle * attended)

        @pl.when(step == seqs * per_seq - 1)
        def _():
            g_out[...] = g_sum[...].astype(BF16)

    row = pl.BlockSpec((block, width), lambda i: (i, 0))
    unit_row = pl.BlockSpec((block, units), lambda i: (i, 0))
    return call(
        kernel,
        "finish_block",
        (rows // block,),
        [smem(), row, row, row, whole((1, width)), whole((1, width)), whole(modulation.shape)]
        + [whole(out_weight.shape), whole((1, width))]
        + [unit_row] * (2 * groups)
        + [whole(ups[0].shape)] * groups
        + [whole(downs[0].shape)] * groups,
        (
            row,
            row,
            row,
            pl.BlockSpec((width, width), lambda i: (0, 0)),
            pl.BlockSpec((1, 8, width), lambda i: (i // per_seq, 0, 0)),
        ),
        (
            jax.ShapeDtypeStruct((rows, width), BF16),
            jax.ShapeDtypeStruct((rows, width), F32),
            jax.ShapeDtypeStruct((rows, width), BF16),
            jax.ShapeDtypeStruct((width, width), BF16),
            jax.ShapeDtypeStruct((seqs, 8, width), F32),
        ),
        [pltpu.VMEM((width, width), F32)],
        rows * width * (4 * units * groups + 6 * width),
        rows * (width * 14 + units * groups * 4) + 4 * width * units * groups,
    )(
        span, mixture, tokens, cot, embed, gain, modulation, out_weight, down_bias,
        *actives, *d_uppers, *ups, *downs,
    )


def weight_grad(turned, grads, tile=256):
    width, rows = turned.shape
    count = len(grads)
    tiles = grads[0].shape[1] // tile

    def kernel(left, *refs):
        out = refs[count]
        which = pl.program_id(0) // tiles
        for part in range(count):

            @pl.when(which == part)
            def _():
                out[...] = mxu(left[...], refs[part][...]).astype(BF16)

    def column(part):
        return pl.BlockSpec(
            (rows, tile), lambda i: (0, jnp.clip(i - part * tiles, 0, tiles - 1))
        )

    return call(
        kernel,
        "weight_grad",
        (count * tiles,),
        [whole(turned.shape)] + [column(part) for part in range(count)],
        pl.BlockSpec((width, tile), lambda i: (0, i)),
        jax.ShapeDtypeStruct((width, count * tiles * tile), BF16),
        [],
        2 * rows * width * count * tiles * tile,
        2 * (rows * width * (count + 1) + count * width * width),
    )(turned, *grads)


def finish_start(tokens, d_middle, d_parts, span, embed, gain, modulation, weight, seqs, block=512):
    rows, width = tokens.shape
    seq_length = rows // seqs
    block = min(block, seq_length)
    per_seq = seq_length // block

    def kernel(span_ref, tok, d_mid, dq, dk, dv, emb, gn, mod, w, g_tok, sums):
        step = pl.program_id(0)
        seq = step // per_seq
        first = (step - seq * per_seq) * block

        @pl.when(step == seq * per_seq)
        def _():
            sums[...] = jnp.zeros_like(sums)

        start, inside = masked_rows(tok[...], emb[...], span_ref[0, seq], span_ref[1, seq], first)
        hat, inverse = normalized(start)
        d_normed = mxu(dq[...], w[:, 0:width], TRANSPOSED)
        d_normed += mxu(dk[...], w[:, width : 2 * width], TRANSPOSED)
        d_normed += mxu(dv[...], w[:, 2 * width :], TRANSPOSED)
        scale = mod[pl.ds(seq, 1), width : 2 * width]
        d_start = d_mid[...] + norm_back(d_normed * (gn[...] * (1.0 + scale)), hat, inverse)
        g_tok[...] = jnp.where(inside, 0.0, d_start)
        sums[0, 0:1, :] += column_sum(d_normed)
        sums[0, 1:2, :] += column_sum(d_normed * hat)
        sums[0, 2:3, :] += column_sum(jnp.where(inside, d_start, 0.0))

    row = pl.BlockSpec((block, width), lambda i: (i, 0))
    return call(
        kernel,
        "finish_start",
        (rows // block,),
        [smem(), row, row, row, row, row, whole((1, width)), whole((1, width))]
        + [whole(modulation.shape), whole(weight.shape)],
        (row, pl.BlockSpec((1, 8, width), lambda i: (i // per_seq, 0, 0))),
        (
            jax.ShapeDtypeStruct((rows, width), F32),
            jax.ShapeDtypeStruct((seqs, 8, width), F32),
        ),
        [],
        2 * rows * width * 3 * width,
        rows * width * 16,
    )(span, tokens, d_middle, *d_parts, embed, gain, modulation, weight)


def gather(v, axis=0):
    return lax.all_gather(v, "narrow", axis=axis, tiled=True)


def reduce_share(v):
    return lax.psum(lax.psum_scatter(v, "narrow", scatter_dimension=0, tiled=True), "wide")


def per_device(
    tokens,
    timestep,
    span_start,
    span_length,
    mask_embed,
    ada_weight,
    ada_bias,
    norm_first,
    query_key_value_weight,
    output_weight,
    norm_second,
    up_projection_weight,
    up_projection_bias,
    down_projection_weight,
    down_projection_bias,
    cotangent,
):
    seqs = timestep.shape[0]
    rows, width = tokens.shape
    seq_length = rows // seqs
    ways = lax.axis_size("narrow")
    share = width // ways
    unit_share = down_projection_weight.shape[0]
    part = unit_share // GROUPS
    units = ways * part

    small = jnp.concatenate(
        [mask_embed, ada_bias, norm_first, norm_second, up_projection_bias, down_projection_bias]
    )
    ada_columns = ada_weight.shape[1]
    filler = -small.shape[0] % ada_columns
    small = jnp.pad(small, (0, filler)).reshape(-1, ada_columns)
    packed = gather(jnp.concatenate([ada_weight, small])[None])
    w_qkv = gather(query_key_value_weight)
    w_out = gather(output_weight)
    up_parts = up_projection_weight.reshape(share, ways, GROUPS, part)
    ups = [gather(up_parts[:, :, group].reshape(share, units)) for group in range(GROUPS)]
    downs = [
        gather(down_projection_weight[group * part : (group + 1) * part]) for group in range(GROUPS)
    ]

    time_width = ada_weight.shape[0]
    ada_full = jnp.moveaxis(packed[:, :time_width], 0, 1).reshape(time_width, -1)
    rest = packed[:, time_width:].reshape(ways, -1)

    def small_part(lower, size):
        return rest[:, lower : lower + size].reshape(1, ways * size)

    spot = 0
    smalls = []
    for size in (share, ada_columns, share, share, unit_share, share):
        smalls.append(small_part(spot, size))
        spot += size
    embed, bias_ada, gain_one, gain_two, bias_up, bias_down = [v.astype(F32) for v in smalls]
    features = time_features(timestep, time_width)
    modulation = jnp.dot(features, ada_full.astype(F32), precision=FULL_PRECISION) + bias_ada
    span = jnp.stack([span_start, span_length])
    tables = rotary_tables(seq_length)

    qkv, turned_one = project(tokens, span, embed, gain_one, modulation, w_qkv, tables, seqs)
    mixture, total = attend(qkv, seqs)
    normed_two = middle_norm(mixture, tokens, span, embed, gain_two, modulation, w_out, seqs)
    bias_parts = bias_up.reshape(ways, GROUPS, part)
    actives, d_uppers, g_ups, g_downs, g_biases = [], [], [], [], []
    for group in range(GROUPS):
        active, d_upper, g_up, g_down, g_bias, g_bias_down = hidden_units(
            normed_two,
            cotangent,
            modulation,
            ups[group],
            bias_parts[:, group].reshape(1, units),
            downs[group],
            seqs,
        )
        actives.append(active)
        d_uppers.append(d_upper)
        g_ups.append(reduce_share(g_up))
        g_downs.append(reduce_share(g_down))
        g_biases.append(g_bias)
    block_out, d_middle, d_mixture, g_out, sums_two = finish_block(
        mixture, tokens, cotangent, span, embed, gain_two, modulation, w_out, bias_down,
        actives, d_uppers, ups, downs, seqs,
    )
    g_out = reduce_share(g_out)
    d_parts = attend_back(qkv, mixture, d_mixture, total, tables, seqs)
    g_qkv = reduce_share(weight_grad(turned_one, d_parts))
    grad_tokens, sums_one = finish_start(
        tokens, d_middle, d_parts, span, embed, gain_one, modulation, w_qkv, seqs
    )

    scale_one = modulation[:, width : 2 * width]
    scale_two = modulation[:, 4 * width : 5 * width]
    d_modulation = jnp.concatenate(
        [
            sums_one[:, 0],
            sums_one[:, 1] * gain_one,
            sums_two[:, 3],
            sums_two[:, 1],
            sums_two[:, 2] * gain_two,
            sums_two[:, 0],
        ],
        axis=1,
    )
    d_modulation = lax.all_to_all(
        d_modulation.reshape(seqs, ways, -1), "narrow", split_axis=1, concat_axis=0, tiled=True
    )[:, 0]
    d_modulation = lax.all_gather(d_modulation, "wide", axis=0, tiled=True)
    steps = lax.all_gather(timestep, ("wide", "narrow"), axis=0, tiled=True)
    grad_ada_weight = lax.dot_general(
        time_features(steps, time_width),
        d_modulation,
        (((0,), (0,)), ((), ())),
        precision=FULL_PRECISION,
    )
    grad_ada_bias = jnp.sum(d_modulation, axis=0)

    g_bias_up = jnp.stack(
        [v.reshape(ways, part) for v in g_biases], axis=1
    ).reshape(ways, unit_share)
    vectors = jnp.concatenate(
        [
            jnp.sum(sums_one[:, 2], axis=0).reshape(ways, share),
            jnp.sum(sums_one[:, 1] * (1.0 + scale_one), axis=0).reshape(ways, share),
            jnp.sum(sums_two[:, 2] * (1.0 + scale_two), axis=0).reshape(ways, share),
            g_bias_up,
            g_bias_down.reshape(ways, share),
        ],
        axis=1,
    )
    vectors = lax.psum(vectors, ("wide", "narrow"))
    own = lax.dynamic_slice_in_dim(vectors, lax.axis_index("narrow"), 1, 0)[0]
    grad_mask_embed = own[:share]
    grad_norm_first = own[share : 2 * share]
    grad_norm_second = own[2 * share : 3 * share]
    grad_up_bias = own[3 * share : 3 * share + unit_share]
    grad_down_bias = own[3 * share + unit_share :]

    grad_up = jnp.stack(
        [v.reshape(share, ways, part) for v in g_ups], axis=2
    ).reshape(share, ways * unit_share)
    grad_down = jnp.concatenate(g_downs)
    return (
        block_out,
        grad_tokens,
        grad_mask_embed,
        grad_ada_weight,
        grad_ada_bias,
        grad_norm_first,
        g_qkv.astype(F32),
        g_out.astype(F32),
        grad_norm_second,
        grad_up.astype(F32),
        grad_up_bias,
        grad_down.astype(F32),
        grad_down_bias,
    )


def solution(mesh):
    rows = P(("wide", "narrow"), None)
    per_seq = P(("wide", "narrow"))
    vector, matrix, columns = P("narrow"), P("narrow", None), P(None, "narrow")
    return jax.shard_map(
        per_device,
        mesh=mesh,
        in_specs=(
            rows, per_seq, per_seq, per_seq, vector, columns, vector, vector,
            matrix, matrix, vector, matrix, vector, matrix, vector, rows,
        ),
        out_specs=(
            rows, rows, vector, columns, vector, vector, matrix, matrix, vector, matrix,
            vector, matrix, vector,
        ),
        check_vma=False,
    )
```

time: 1530 us -> 681 us (0.45)
  matrix products: 543 us -> 3.27 us
  Pallas kernels: 0 us -> 289 us
  waiting for transfers between devices: 415 us -> 183 us
  local copies, waits for them, and re-layouts: 250 us -> 39.2 us
  other arithmetic: 210 us -> 23.2 us
  blocking collectives: 69.6 us -> 117 us
    dot_general x54 -> x2, matrix products: 543 us -> 3.27 us  [the longest x1 1.7 us: per_device(): jnp.dot(features, ada_full.astype(F32), precision=FULL_PRECISION) + bias_ada]
    pallas_call x0 -> x10, Pallas kernels: none -> 289 us  [the longest x1 81.7 us: attend_back(): call(kernel, 'attend_back', (seqs, steps), [part_of(0), part_of(1), part_...]
    psum x1, waiting for transfers between devices: 198 us -> 29.6 us  [reduce_share(): lax.psum(lax.psum_scatter(v, 'narrow', scatter_dimension=0, tiled=True),...]
    reduce_scatter x5 -> x8, waiting for transfers between devices: 202 us -> 78.9 us  [reduce_share(): lax.psum_scatter(v, 'narrow', scatter_dimension=0, tiled=True)]
    dynamic_update_slice x8 -> x0, local copies, waits for them, and re-layouts: 122 us -> none  [per_sequence(): lax.scan(per_block, (zeros_init, zeros_init), (query_blocks, grad_blocks,...]
    convert_element_type x12 -> x9, other arithmetic: 97.5 us -> 10.2 us  [the longest x1 2.89 us: per_device(): grad_up.astype(F32)]
    all_gather x5 -> x9, waiting for transfers between devices: 11 us -> 70.3 us  [gather(): return lax.all_gather(v, 'narrow', axis=axis, tiled=True)]
    reduce_sum x12 -> x3, other arithmetic: 56.6 us -> 2.75 us  [the longest x1 1.31 us: per_device(): jnp.sum(sums_two[:, 2] * (1.0 + scale_two), axis=0).reshape(ways, share)]
  transfers between devices with their start and end apart: 11 -> 19, of which waited for: 5 -> 9; matrix products, arithmetic and copies ran while one was open for 26% -> 7% of each run, Pallas kernels for 0% -> 43%
where the time goes in v1:
time: 681 us; the launch traced here: 674 us
  Pallas kernels  289 us (42%)
  waiting for transfers between devices  183 us (27%)
  blocking collectives  117 us (17%)
  local copies, waits for them, and re-layouts  39.2 us (6%)
  other arithmetic  23.2 us (3%)
  between operations  15.2 us (2%)
    pallas_call x1, Pallas kernels, attend_back(): call(kernel, 'attend_back', (seqs, steps), [part_of(0), part_of(1), part_...  81.7 us
    reduce_scatter x8, waiting for transfers between devices, reduce_share(): lax.psum_scatter(v, 'narrow', scatter_dimension=0, tiled=True)  78.9 us
    all_gather x9, waiting for transfers between devices, gather(): return lax.all_gather(v, 'narrow', axis=axis, tiled=True)  70.3 us
    pallas_call x3, Pallas kernels, hidden_units(): call(kernel, 'hidden_units', (steps + tiles,), [pl.BlockSpec((block, widt...  65.7 us
    pallas_call x1, Pallas kernels, finish_block(): call(kernel, 'finish_block', (rows // block,), [smem(), row, row, row, wh...  50 us
    unnamed x1, blocking collectives  42.9 us
    psum x1, blocking collectives, per_device(): vectors = lax.psum(vectors, ('wide', 'narrow'))  41.9 us
    pallas_call x1, Pallas kernels, attend(): call(kernel, 'attend', (seqs, steps), [part_of(0), part_of(1), part_of(2)...  37.4 us
  transfers between devices with their start and end apart: 19, of which 9 were waited for; matrix products, arithmetic and copies ran while one was open for 7% of the time, Pallas kernels for 43%

profile of v1, /device:TPU:0, one launch (start us, length us, event | category | flops | bytes accessed | tf_op | source)
XLA Modules:
  0.0 674.1 jit_solution(7476680629598090854)
XLA Ops:
  7.2 4.2 concatenate.30
  17.7 5.4 slice_reduce_fusion
  40.9 25.5 %all-gather.12.cloned.1.call-done.w = bf16[768,2304]{1,0:T(8,128)(2,1)} async-done(((bf16[192,2304]{1,0:T(8,128)(2,1)}), bf16[768,2304]{1,0:T(8,128)(2,1)}) %all-gather.12.cloned.1.call-update) | async-done | bytes 3538960 | tf_op jit(solution)/shard_map/all_gather | solution.py:616
  66.4 14.6 %project.1 = (bf16[2048,2304]{1,0:T(8,128)(2,1)}, bf16[768,2048]{1,0:T(8,128)(2,1)}) custom-call(s32[2,2]{1,0:T(2,128)} %pad_add_fusion.span_ref.refs_0_, bf16[2048,768]{1,0:T(8,128)(2,1)} %tok.5, f32[1,768]{1,0:T(1,128)} %reshape.171.emb.refs_4_, f32[1,768]{1,0:T(1,128)} %reshape.172.gn, f32[2,4608]{1,0:T(2,128)} %convolution_add_fusion.mod.refs_6_, ...), custom_call_target="tpu_custom_call" | custom-call | flops 7247757312 | bytes 19267584 | tf_op jit(solution)/shard_map/project/pallas_call | solution.py:128
  81.0 37.4 %attend.1 = (bf16[2048,768]{1,0:T(8,128)(2,1)}, f32[2,6,2,1024]{3,2,1,0:T(2,128)}) custom-call(bf16[2048,2304]{1,0:T(8,128)(2,1)} %get-tuple-element.43.q_ref.k_ref.v_ref, bf16[2048,2304]{1,0:T(8,128)(2,1)} %get-tuple-element.43.q_ref.k_ref.v_ref, bf16[2048,2304]{1,0:T(8,128)(2,1)} %get-tuple-element.43.q_ref.k_ref.v_ref), custom_call_target="tpu_custom_call" | custom-call | flops 25769803776 | bytes 12582912 | tf_op jit(solution)/shard_map/attend/pallas_call | solution.py:216
  118.3 8.2 %middle_norm.1.nrm = bf16[2048,768]{1,0:T(8,128)(2,1)} custom-call(s32[2,2]{1,0:T(2,128)} %pad_add_fusion.span_ref.refs_0_, bf16[2048,768]{1,0:T(8,128)(2,1)} %get-tuple-element.44.mix.refs_1_, bf16[2048,768]{1,0:T(8,128)(2,1)} %tok.5, f32[1,768]{1,0:T(1,128)} %reshape.171.emb.refs_4_, f32[1,768]{1,0:T(1,128)} %reshape.174.gn.refs_5_, ...), custom_call_target="tpu_custom_call" | custom-call | flops 2415919104 | bytes 9437184 | tf_op jit(solution)/shard_map/middle_norm/pallas_call | solution.py:334
  128.3 21.8 %hidden_units.5 = (bf16[2048,1024]{1,0:T(8,128)(2,1)}, bf16[2048,1024]{1,0:T(8,128)(2,1)}, bf16[768,1024]{1,0:T(8,128)(2,1)}, bf16[1024,768]{1,0:T(8,128)(2,1)}, f32[1,1024]{1,0:T(1,128)}, /*index=5*/f32[1,768]{1,0:T(1,128)}) custom-call(bf16[2048,768]{1,0:T(8,128)(2,1)} %middle_norm.1.nrm, bf16[2048,768]{1,0:T(8,128)(2,1)} %refs_3_.1, ...), custom_call_target="tpu_custom_call" | custom-call | flops 12884901888 | bytes 20971520 | tf_op jit(solution)/shard_map/hidden_units/pallas_call | solution.py:405
  150.8 20.4 %all-gather.20.cloned.1.call-done.w_up.refs_16_ = bf16[768,1024]{1,0:T(8,128)(2,1)} async-done(((bf16[192,1024]{1,0:T(8,128)(2,1)}), bf16[768,1024]{1,0:T(8,128)(2,1)}) %all-gather.20.cloned.1.call-update) | async-done | bytes 1572880 | tf_op jit(solution)/shard_map/all_gather | solution.py:616
  171.2 22.1 %hidden_units.4 = (bf16[2048,1024]{1,0:T(8,128)(2,1)}, bf16[2048,1024]{1,0:T(8,128)(2,1)}, bf16[768,1024]{1,0:T(8,128)(2,1)}, bf16[1024,768]{1,0:T(8,128)(2,1)}, f32[1,1024]{1,0:T(1,128)}, /*index=5*/f32[1,768]{1,0:T(1,128)}) custom-call(bf16[2048,768]{1,0:T(8,128)(2,1)} %middle_norm.1.nrm, bf16[2048,768]{1,0:T(8,128)(2,1)} %refs_3_.1, ...), custom_call_target="tpu_custom_call" | custom-call | flops 12884901888 | bytes 20971520 | tf_op jit(solution)/shard_map/hidden_units/pallas_call | solution.py:405
  194.0 20.9 %all-gather.16.cloned.1.call-done.w_up.refs_15_ = bf16[768,1024]{1,0:T(8,128)(2,1)} async-done(((bf16[192,1024]{1,0:T(8,128)(2,1)}), bf16[768,1024]{1,0:T(8,128)(2,1)}) %all-gather.16.cloned.1.call-update) | async-done | bytes 1572880 | tf_op jit(solution)/shard_map/all_gather | solution.py:616
  214.9 21.8 %hidden_units.3 = (bf16[2048,1024]{1,0:T(8,128)(2,1)}, bf16[2048,1024]{1,0:T(8,128)(2,1)}, bf16[768,1024]{1,0:T(8,128)(2,1)}, bf16[1024,768]{1,0:T(8,128)(2,1)}, f32[1,1024]{1,0:T(1,128)}, /*index=5*/f32[1,768]{1,0:T(1,128)}) custom-call(bf16[2048,768]{1,0:T(8,128)(2,1)} %middle_norm.1.nrm, bf16[2048,768]{1,0:T(8,128)(2,1)} %refs_3_.1, ...), custom_call_target="tpu_custom_call" | custom-call | flops 12884901888 | bytes 20971520 | tf_op jit(solution)/shard_map/hidden_units/pallas_call | solution.py:405
  237.5 50.0 %finish_block.1 = (bf16[2048,768]{1,0:T(8,128)(2,1)}, f32[2048,768]{1,0:T(8,128)}, bf16[2048,768]{1,0:T(8,128)(2,1)}, bf16[768,768]{1,0:T(8,128)(2,1)}, f32[2,8,768]{2,1,0:T(8,128)}) custom-call(s32[2,2]{1,0:T(2,128)} %pad_add_fusion.span_ref.refs_0_, bf16[2048,768]{1,0:T(8,128)(2,1)} %get-tuple-element.44.mix.refs_1_, bf16[2048,768]{1,0:T(8,128)(2,1)} %tok.5, ...), custom_call_target="tpu_custom_call" | custom-call | flops 26575110144 | bytes 56623104 | tf_op jit(solution)/shard_map/finish_block/pallas_call | solution.py:506
  289.3 81.7 %attend_back.1 = (bf16[2048,768]{1,0:T(8,128)(2,1)}, bf16[2048,768]{1,0:T(8,128)(2,1)}, bf16[2048,768]{1,0:T(8,128)(2,1)}) custom-call(bf16[2048,2304]{1,0:T(8,128)(2,1)} %get-tuple-element.43.q_ref.k_ref.v_ref, bf16[2048,2304]{1,0:T(8,128)(2,1)} %get-tuple-element.43.q_ref.k_ref.v_ref, bf16[2048,2304]{1,0:T(8,128)(2,1)} %get-tuple-element.43.q_ref.k_ref.v_ref, ...), custom_call_target="tpu_custom_call" | custom-call | flops 64424509440 | bytes 25165824 | tf_op jit(solution)/shard_map/attend_back/pallas_call | solution.py:292
  371.0 14.1 %weight_grad.1 = bf16[768,2304]{1,0:T(8,128)(2,1)} custom-call(bf16[768,2048]{1,0:T(8,128)(2,1)} %get-tuple-element.65.left, bf16[2048,768]{1,0:T(8,128)(2,1)} %get-tuple-element.55.dq.refs_0_, bf16[2048,768]{1,0:T(8,128)(2,1)} %get-tuple-element.56.dk.refs_1_, bf16[2048,768]{1,0:T(8,128)(2,1)} %get-tuple-element.57.dv.refs_2_), custom_call_target="tpu_custom_call" | custom-call | flops 7247757312 | bytes 16121856 | tf_op jit(solution)/shard_map/weight_grad/pallas_call | solution.py:557
  385.2 3.1 stack_reshape.26
  394.0 4.0 reduce-scatter.21.cloned.1.call-done
  398.0 31.2 %reduce-scatter.19.cloned.1.call-done = bf16[256,768]{1,0:T(8,128)(2,1)} async-done(((bf16[1024,768]{1,0:T(8,128)(2,1)}), bf16[256,768]{1,0:T(8,128)(2,1)}) %reduce-scatter.19.cloned.1.call-update) | async-done | bytes 393232 | tf_op jit(solution)/shard_map/reduce_scatter | solution.py:620
  429.2 43.6 %reduce-scatter.9.cloned.1.call-done = bf16[192,2304]{1,0:T(8,128)(2,1)} async-done(((bf16[768,2304]{1,0:T(8,128)(2,1)}), bf16[192,2304]{1,0:T(8,128)(2,1)}) %reduce-scatter.9.cloned.1.call-update) | async-done | bytes 884752 | tf_op jit(solution)/shard_map/reduce_scatter | solution.py:620
  473.6 42.9 %all-reduce.1 = s32[64]{0:T(128)S(1)} all-reduce(s32[64]{0:T(128)S(1)} %dynamic-update-slice), channel_id=1, replica_groups=mesh['wide'=8,'narrow'=4] {'wide','narrow'}, use_global_device_ids=true, to_apply=%add.1 | all-reduce | flops 64 | bytes 512
  519.6 17.4 %finish_start.1 = (f32[2048,768]{1,0:T(8,128)}, f32[2,8,768]{2,1,0:T(8,128)}) custom-call(s32[2,2]{1,0:T(2,128)} %pad_add_fusion.span_ref.refs_0_, bf16[2048,768]{1,0:T(8,128)(2,1)} %tok.5, f32[2048,768]{1,0:T(8,128)} %get-tuple-element.52.d_mid, bf16[2048,768]{1,0:T(8,128)(2,1)} %get-tuple-element.55.dq.refs_0_, ...), custom_call_target="tpu_custom_call" | custom-call | flops 7247757312 | bytes 25165824 | tf_op jit(solution)/shard_map/finish_start/pallas_call | solution.py:598
  543.1 3.6 all-to-all-start
  546.8 41.9 %psum.63 = f32[4,1536]{1,0:T(4,128)S(1)} all-reduce(f32[4,1536]{1,0:T(4,128)S(1)} %concatenate.36), channel_id=1, replica_groups=mesh['wide'=8,'narrow'=4] {'wide','narrow'}, use_global_device_ids=true, to_apply=%region_3.4 | all-reduce | flops 6144 | bytes 49152 | tf_op jit(solution)/shard_map/psum | solution.py:753
  590.1 32.0 %all_gather.43 = f32[64,1152]{1,0:T(8,128)S(1)} all-gather(f32[8,1152]{1,0:T(8,128)S(1)} %squeeze.31), channel_id=1, replica_groups=mesh['wide'=8,'narrow'=4] {'wide'}, dimensions={0}, use_global_device_ids=true | all-gather | bytes 331776 | tf_op jit(solution)/shard_map/all_gather | solution.py:730
  624.3 29.6 %all-reduce.5.cloned.1.call-done = (bf16[192,2304]{1,0:T(8,128)(2,1)}, bf16[192,768]{1,0:T(8,128)(2,1)}, bf16[192,4,1,256]{3,2,1,0:T(2,128)(2,1)}, bf16[192,4,1,...) async-done(((bf16[192,2304]{1,0:T(8,128)(2,1)}, ...) | async-done | bytes 3538960 | tf_op jit(solution)/shard_map/psum | solution.py:620
  (166 shorter events, 61.5 us)
Async XLA Ops:
  7.2 26.9 %all-gather.28.cloned.1.call-start = ((), (), s32[]{:S(2)}) async-start(), calls=%async_computation.25 | async-start | bytes 1566720 | tf_op jit(solution)/shard_map/all_gather | solution.py:616
  13.3 53.1 %all-gather.12.cloned.1.call-start = ((), (), s32[]{:S(2)}) async-start(), calls=%async_computation.9 | async-start | bytes 4423680 | tf_op jit(solution)/shard_map/all_gather | solution.py:616
  14.1 104.3 %all-gather.14.cloned.1.call-start = ((), (), s32[]{:S(2)}) async-start(), calls=%async_computation.10 | async-start | bytes 1474560 | tf_op jit(solution)/shard_map/all_gather | solution.py:616
  14.8 111.8 %all-gather.26.cloned.1.call-start = ((), (), s32[]{:S(2)}) async-start(), calls=%async_computation.16 | async-start | bytes 1966080 | tf_op jit(solution)/shard_map/all_gather | solution.py:616
  15.9 112.4 %all-gather.24.cloned.1.call-start = ((), (), s32[]{:S(2)}) async-start(), calls=%async_computation.15 | async-start | bytes 1966080 | tf_op jit(solution)/shard_map/all_gather | solution.py:616
  24.0 126.8 %all-gather.22.cloned.1.call-start = ((), (), s32[]{:S(2)}) async-start(), calls=%async_computation.14 | async-start | bytes 1966080 | tf_op jit(solution)/shard_map/all_gather | solution.py:616
  24.6 146.7 %all-gather.20.cloned.1.call-start = ((), (), s32[]{:S(2)}) async-start(), calls=%async_computation.13 | async-start | bytes 1966080 | tf_op jit(solution)/shard_map/all_gather | solution.py:616
  25.4 168.6 %all-gather.18.cloned.1.call-start = ((), (), s32[]{:S(2)}) async-start(), calls=%async_computation.12 | async-start | bytes 1966080 | tf_op jit(solution)/shard_map/all_gather | solution.py:616
  26.2 188.7 %all-gather.16.cloned.1.call-start = ((), (), s32[]{:S(2)}) async-start(), calls=%async_computation.11 | async-start | bytes 1966080 | tf_op jit(solution)/shard_map/all_gather | solution.py:616
  27.1 358.1 %reduce-scatter.17.cloned.1.call-start = ((), (), s32[]{:S(2)}) async-start(), calls=%async_computation.21 | async-start | bytes 1966080 | tf_op jit(solution)/shard_map/reduce_scatter | solution.py:620
  150.2 238.1 %reduce-scatter.15.cloned.1.call-start = ((), (), s32[]{:S(2)}) async-start(), calls=%async_computation.20 | async-start | bytes 1966080 | tf_op jit(solution)/shard_map/reduce_scatter | solution.py:620
  193.3 197.8 %reduce-scatter.13.cloned.1.call-start = ((), (), s32[]{:S(2)}) async-start(), calls=%async_computation.19 | async-start | bytes 1966080 | tf_op jit(solution)/shard_map/reduce_scatter | solution.py:620
  236.7 157.2 %reduce-scatter.11.cloned.1.call-start = ((), (), s32[]{:S(2)}) async-start(), calls=%async_computation.18 | async-start | bytes 1474560 | tf_op jit(solution)/shard_map/reduce_scatter | solution.py:620
  287.5 106.4 %reduce-scatter.23.cloned.1.call-start = ((), (), s32[]{:S(2)}) async-start(), calls=%async_computation.24 | async-start | bytes 1966080 | tf_op jit(solution)/shard_map/reduce_scatter | solution.py:620
  288.1 109.9 %reduce-scatter.21.cloned.1.call-start = ((), (), s32[]{:S(2)}) async-start(), calls=%async_computation.23 | async-start | bytes 1966080 | tf_op jit(solution)/shard_map/reduce_scatter | solution.py:620
  288.7 140.5 %reduce-scatter.19.cloned.1.call-start = ((), (), s32[]{:S(2)}) async-start(), calls=%async_computation.22 | async-start | bytes 1966080 | tf_op jit(solution)/shard_map/reduce_scatter | solution.py:620
  289.3 183.5 %reduce-scatter.9.cloned.1.call-start = ((), (), s32[]{:S(2)}) async-start(), calls=%async_computation.17 | async-start | bytes 4423680 | tf_op jit(solution)/shard_map/reduce_scatter | solution.py:620
  385.1 268.8 %all-reduce.5.cloned.1.call-start = ((), (), s32[]{:S(2)}) async-start(), calls=%async_computation.26 | async-start | bytes 9437184 | tf_op jit(solution)/shard_map/psum | solution.py:620
  472.8 44.6 %copy-start.11 = (f32[1,1024]{1,0:T(1,128)S(1)}, f32[1,1024]{1,0:T(1,128)}, u32[]{:S(2)}) copy-start(f32[1,1024]{1,0:T(1,128)} %get-tuple-element.63) | copy-start | bytes 12292
  472.8 45.3 %copy-start.14 = (f32[1,768]{1,0:T(1,128)S(1)}, f32[1,768]{1,0:T(1,128)}, u32[]{:S(2)}) copy-start(f32[1,768]{1,0:T(1,128)} %get-tuple-element.64) | copy-start | bytes 9220
  472.8 45.4 %copy-start.12 = (f32[1,1024]{1,0:T(1,128)S(1)}, f32[1,1024]{1,0:T(1,128)}, u32[]{:S(2)}) copy-start(f32[1,1024]{1,0:T(1,128)} %get-tuple-element.62) | copy-start | bytes 12292
  472.8 46.1 %copy-start.13 = (f32[1,1024]{1,0:T(1,128)S(1)}, f32[1,1024]{1,0:T(1,128)}, u32[]{:S(2)}) copy-start(f32[1,1024]{1,0:T(1,128)} %get-tuple-element.61) | copy-start | bytes 12292
  472.8 46.7 %copy-start.6 = (f32[2,8,768]{2,1,0:T(8,128)S(1)}, f32[2,8,768]{2,1,0:T(8,128)}, u32[]{:S(2)}) copy-start(f32[2,8,768]{2,1,0:T(8,128)} %get-tuple-element.60) | copy-start | bytes 147460
  543.1 46.9 %all-to-all-start = ((f32[2,4,1152]{2,0,1:T(2,128)}), f32[2,4,1152]{2,0,1:T(2,128)S(1)}, u32[]{:S(2)}, u32[]{:S(2)}) async-start(f32[2,4,1152]{2,0,1:T(2,128)} %bitcast.15), calls=%async_computation | async-start | bytes 73728 | tf_op jit(solution)/shard_map/all_to_all | solution.py:727
  (17 other events, 185.0 us)
Sparse Core Ops, SparseCore 0:
  13.4 20.5 all-gather.27
  35.6 30.7 all-gather.11
  68.0 17.4 all-gather.13
  87.5 19.6 all-gather.25
  108.6 19.6 all-gather.23
  130.3 19.6 all-gather.21
  151.5 19.6 all-gather.19
  173.4 19.6 all-gather.17
  195.2 19.6 all-gather.15
  217.3 28.1 reduce-scatter.16
  248.8 28.1 reduce-scatter.14
  279.9 28.1 reduce-scatter.12
  310.9 25.7 reduce-scatter.10
  339.1 28.1 reduce-scatter.22
  369.8 28.1 reduce-scatter.20
  401.0 28.1 reduce-scatter.18
  432.3 40.4 reduce-scatter.8
  478.2 175.5 all-reduce.4

commit v2 on v1

v2 whole, which is shorter than its diff:
```python
import math

import jax
import jax.numpy as jnp
from jax import lax
from jax.experimental import pallas as pl
from jax.experimental.pallas import tpu as pltpu
from jax.sharding import PartitionSpec as P

HEAD = 64
PAIR = 2 * HEAD
GROUPS = 3
EPSILON = 1e-05
FULL_PRECISION = lax.Precision.HIGHEST
F32 = jnp.float32
BF16 = jnp.bfloat16
SCALE = 1.0 / math.sqrt(HEAD)
SCALE2 = SCALE * math.log2(math.e)
VMEM_BYTES = 60 << 20
PLAIN = (((1,), (0,)), ((), ()))
TRANSPOSED = (((1,), (1,)), ((), ()))


def mxu(left, right, dims=PLAIN):
    return lax.dot_general(left, right, dims, preferred_element_type=F32)


def call(
    kernel, name, grid, in_specs, out_specs, out_shape, scratch, flops, moved, exps=0, ident=None
):
    return pl.pallas_call(
        kernel,
        name=name,
        grid=grid,
        in_specs=in_specs,
        out_specs=out_specs,
        out_shape=out_shape,
        scratch_shapes=scratch,
        compiler_params=pltpu.CompilerParams(
            vmem_limit_bytes=VMEM_BYTES, collective_id=ident, has_side_effects=ident is not None
        ),
        cost_estimate=pl.CostEstimate(flops=flops, bytes_accessed=moved, transcendentals=exps),
    )


def whole(shape):
    return pl.BlockSpec(shape, lambda *_: (0,) * len(shape), pipeline_mode=pl.Buffered(1))


def smem():
    return pl.BlockSpec(memory_space=pltpu.SMEM)


def time_features(step_ids, feature_count):
    halfway = feature_count // 2
    spacing = jnp.exp(-math.log(10000.0) * jnp.arange(halfway, dtype=F32) / halfway)
    angles = step_ids.astype(F32)[:, None] * spacing[None, :]
    return jax.nn.silu(jnp.concatenate([jnp.cos(angles), jnp.sin(angles)], axis=-1))


def rotary_tables(seq_length):
    halfway = HEAD // 2
    spacing = jnp.exp(-math.log(10000.0) * jnp.arange(halfway, dtype=F32) / halfway)
    angles = jnp.arange(seq_length, dtype=F32)[:, None] * spacing[None, :]
    cosine, sine = jnp.cos(angles), jnp.sin(angles)
    nothing = jnp.zeros_like(sine)
    cosines = jnp.concatenate([cosine] * 4, axis=-1)
    upper = jnp.concatenate([-sine, nothing] * 2, axis=-1)
    lower = jnp.concatenate([nothing, sine] * 2, axis=-1)
    return cosines, upper, lower


def from_ahead(v):
    return pltpu.roll(v, PAIR - HEAD // 2, 1)


def from_behind(v):
    return pltpu.roll(v, HEAD // 2, 1)


def masked_rows(tokens, embed, start, length, first_row):
    rows = tokens.shape[0]
    position = lax.broadcasted_iota(jnp.int32, (rows, 1), 0) + first_row
    inside = (position >= start) & (position < start + length)
    return jnp.where(inside, embed, tokens.astype(F32)), inside


def normalized(rows):
    centre = rows - jnp.mean(rows, axis=-1, keepdims=True)
    spread = jnp.mean(centre * centre, axis=-1, keepdims=True)
    inverse = lax.rsqrt(spread + EPSILON)
    return centre * inverse, inverse


def norm_back(d_out, hat, inverse):
    return inverse * (
        d_out
        - jnp.mean(d_out, axis=-1, keepdims=True)
        - hat * jnp.mean(d_out * hat, axis=-1, keepdims=True)
    )


def column_sum(v):
    return jnp.sum(v, axis=0, keepdims=True)


def store_shares(target, value, order_ref, cols):
    count = order_ref.shape[1]
    share = value.shape[0] // count
    for index in range(count):
        spot = pl.ds(pl.multiple_of(order_ref[1, index] * share, share), share)
        target[spot, cols] = value[index * share : (index + 1) * share, :]


def project(tokens, span, order, embed, gain, modulation, weights, tables, seqs, block=512):
    rows, width = tokens.shape
    seq_length = rows // seqs
    block = min(block, seq_length)
    per_seq = seq_length // block
    pairs = width // PAIR

    def kernel(span_ref, order_ref, tok, emb, gn, mod, w_q, w_k, w_v, cos, upp, low, out, nt):
        step = pl.program_id(0)
        seq = step // per_seq
        first = (step - seq * per_seq) * block
        start, _ = masked_rows(tok[...], emb[...], span_ref[0, seq], span_ref[1, seq], first)
        hat, _ = normalized(start)
        shift = mod[pl.ds(seq, 1), 0:width]
        scale = mod[pl.ds(seq, 1), width : 2 * width]
        normed = (hat * (gn[...] * (1.0 + scale)) + shift).astype(BF16)
        store_shares(nt, jnp.transpose(normed), order_ref, slice(None))
        for which, w in enumerate((w_q, w_k)):
            turned = mxu(normed, w[...])
            for part in range(pairs):
                v = turned[:, part * PAIR : (part + 1) * PAIR]
                v = v * cos[...] + from_ahead(v) * upp[...] + from_behind(v) * low[...]
                lower = which * width + part * PAIR
                out[:, lower : lower + PAIR] = v.astype(BF16)
        out[:, 2 * width :] = mxu(normed, w_v[...]).astype(BF16)

    table = pl.BlockSpec((block, PAIR), lambda i: (lax.rem(i, per_seq), 0))
    return call(
        kernel,
        "project",
        (rows // block,),
        [
            smem(),
            smem(),
            pl.BlockSpec((block, width), lambda i: (i, 0)),
            whole((1, width)),
            whole((1, width)),
            whole(modulation.shape),
            whole((width, width)),
            whole((width, width)),
            whole((width, width)),
            table,
            table,
            table,
        ],
        (
            pl.BlockSpec((block, 3 * width), lambda i: (i, 0)),
            pl.BlockSpec((width, block), lambda i: (0, i)),
        ),
        (
            jax.ShapeDtypeStruct((rows, 3 * width), BF16),
            jax.ShapeDtypeStruct((width, rows), BF16),
        ),
        [],
        2 * rows * width * 3 * width,
        rows * width * 10 + 6 * width * width,
    )(span, order, tokens, embed, gain, modulation, *weights, *tables)


def flip(index, stride):
    return index + stride * (1 - 2 * lax.rem(index // stride, 2))


def exchange_stages():
    count = lax.axis_size("wide")
    strides = [1 << bit for bit in range(1, count.bit_length() - 1)]
    return [("pair", "narrow", 1), ("chip", "narrow", 2), ("split", "wide", 1)] + [
        ("full", "wide", stride) for stride in strides
    ] + [("join", "wide", 1)]


class Steps:
    def in_specs(self):
        return [pl.BlockSpec(memory_space=pl.ANY)] * self.count

    out_specs = in_specs

    def locate(self):
        self.at = {axis: lax.axis_index(axis) for axis in ("wide", "narrow")}
        self.odd = lax.rem(self.at["wide"], 2)

    def half_of(self, rows, which, lower=0):
        side = self.odd if which == 0 else 1 - self.odd
        return pl.ds(pl.multiple_of(lower + side * (rows // 2), rows // 2), rows // 2)

    def greet(self):
        barrier = pltpu.get_barrier_semaphore()
        for axis, stride in self.partners:
            pl.semaphore_signal(
                barrier,
                inc=1,
                device_id={axis: flip(self.at[axis], stride)},
                device_id_type=pl.DeviceIdType.MESH,
            )
        pl.semaphore_wait(barrier, len(self.partners))

    def push(self, source, target, sent, got, axis, stride):
        return pltpu.make_async_remote_copy(
            src_ref=source,
            dst_ref=target,
            send_sem=sent,
            recv_sem=got,
            device_id={axis: flip(self.at[axis], stride)},
            device_id_type=pl.DeviceIdType.MESH,
        )

    def tick(self, now, last):
        planned = sorted(self.plan(), key=lambda item: item[:3])
        for when in sorted({item[0] for item in planned if item[0] < last}):

            @pl.when(now == when)
            def _(when=when):
                if when == 0:
                    self.greet()
                for item in planned:
                    if item[0] == when:
                        item[3]()

    def rest(self, last):
        for item in sorted(self.plan(), key=lambda item: item[:3]):
            if item[0] >= last:
                item[3]()


class Gather(Steps):
    partners = (("narrow", 1), ("narrow", 2), ("wide", 1))

    def __init__(self, shapes, begins, waits):
        self.shapes, self.begins, self.waits = shapes, begins, waits
        self.count = len(shapes)

    def out_shape(self):
        return [jax.ShapeDtypeStruct((4 * rows, cols), BF16) for rows, cols in self.shapes]

    def scratch(self):
        dma = pltpu.SemaphoreType.DMA
        return [dma((5,)), dma((5,)), dma((1,))] * self.count

    def bind(self, ins, outs, held):
        self.refs = [(ins[k], outs[k]) + tuple(held[3 * k : 3 * k + 3]) for k in range(self.count)]
        self.locate()

    def block(self, k, index, which=None):
        rows = self.shapes[k][0]
        if which is None:
            return pl.ds(pl.multiple_of(index * rows, rows), rows)
        return self.half_of(rows, which, index * rows)

    def remote(self, k, step):
        source, out, sent, got, _ = self.refs[k]
        me, across = self.at["narrow"], flip(self.at["narrow"], 2)
        axis, stride = (("narrow", 1), ("narrow", 2), ("wide", 1), ("narrow", 1), ("narrow", 1))[step]
        if step == 0:
            ends = (source, out.at[self.block(k, me), :])
        elif step == 1:
            half = self.half_of(self.shapes[k][0], 0)
            ends = (source.at[half, :], out.at[self.block(k, me, 0), :])
        else:
            spot = self.block(k, across, 1 if step == 4 else 0)
            ends = (out.at[spot, :], out.at[spot, :])
        return self.push(*ends, sent.at[step], got.at[step], axis, stride)

    def local(self, k):
        source, out, _, _, near = self.refs[k]
        return pltpu.make_async_copy(
            source, out.at[self.block(k, self.at["narrow"]), :], near.at[0]
        )

    def begin(self, k):
        self.remote(k, 1).start()
        self.remote(k, 0).start()
        self.local(k).start()

    def relay(self, k):
        self.remote(k, 1).wait()
        self.remote(k, 2).start()
        self.remote(k, 3).start()

    def share(self, k):
        self.remote(k, 2).wait()
        self.remote(k, 4).start()

    def close(self, k):
        self.remote(k, 0).wait()
        self.remote(k, 3).wait()
        self.remote(k, 4).wait()
        self.local(k).wait()

    def plan(self):
        planned = []
        for k in range(self.count):
            when = self.begins[k]
            planned.append((when, 0, k, lambda k=k: self.begin(k)))
            for wait, act in zip(self.waits, (self.relay, self.share, self.close)):
                when += wait
                planned.append((when, 1, k, lambda k=k, act=act: act(k)))
        return planned


class Exchange(Steps):
    def __init__(self, shapes, times):
        self.stages = exchange_stages()
        self.shapes = [shape[1:] for shape in shapes]
        self.times = times
        self.count = len(shapes)
        self.partners = sorted({(axis, stride) for _, axis, stride in self.stages})

    def out_shape(self):
        return [jax.ShapeDtypeStruct(shape, BF16) for shape in self.shapes]

    def scratch(self):
        held = []
        for rows, cols in self.shapes:
            held += [
                pltpu.VMEM((2, rows, cols), BF16),
                pltpu.VMEM((2, rows, cols), BF16),
                pltpu.VMEM((rows, cols), BF16),
                pltpu.VMEM((len(self.stages) - 3, rows // 2, cols), BF16),
                pltpu.VMEM((rows // 2, cols), BF16),
                pltpu.SemaphoreType.DMA((len(self.stages),)),
                pltpu.SemaphoreType.DMA((len(self.stages),)),
                pltpu.SemaphoreType.DMA((2,)),
            ]
        return held

    def bind(self, ins, outs, held):
        self.refs = [
            (ins[k], outs[k]) + tuple(held[8 * k : 8 * k + 8]) for k in range(self.count)
        ]
        self.locate()

    def remote(self, k, step):
        source, out, pair, kept, chip, halves, mine, sent, got, _ = self.refs[k]
        kind, axis, stride = self.stages[step]
        rows = self.shapes[k][0]
        if kind == "pair":
            ends = (source.at[0:2], pair)
        elif kind == "chip":
            ends = (kept.at[0], chip)
        elif kind == "split":
            ends = (kept.at[1, self.half_of(rows, 1), :], halves.at[0])
        elif kind == "full":
            ends = (mine, halves.at[step - 2])
        else:
            ends = (mine, out.at[self.half_of(rows, 0), :])
        return self.push(*ends, sent.at[step], got.at[step], axis, stride)

    def local(self, k, which):
        source, out, _, kept, _, _, mine, _, _, near = self.refs[k]
        if which == 0:
            return pltpu.make_async_copy(source.at[2:4], kept, near.at[0])
        half = self.half_of(self.shapes[k][0], 0)
        return pltpu.make_async_copy(mine, out.at[half, :], near.at[1])

    def start(self, k, step):
        self.remote(k, step).start()
        if step == 0:
            self.local(k, 0).start()
        if step == len(self.stages) - 1:
            self.local(k, 1).start()

    def end(self, k, step):
        _, _, pair, kept, chip, halves, mine, _, _, _ = self.refs[k]
        kind = self.stages[step][0]
        self.remote(k, step).wait()
        if kind == "pair":
            self.local(k, 0).wait()
            kept[...] = (kept[...].astype(F32) + pair[...].astype(F32)).astype(BF16)
        elif kind == "chip":
            kept[1] = (kept[1].astype(F32) + chip[...].astype(F32)).astype(BF16)
        elif kind == "split":
            own = self.half_of(self.shapes[k][0], 0)
            mine[...] = (kept[1, own, :].astype(F32) + halves[0].astype(F32)).astype(BF16)
        elif kind == "full":
            mine[...] = (mine[...].astype(F32) + halves[step - 2].astype(F32)).astype(BF16)
        else:
            self.local(k, 1).wait()
        if step + 1 < len(self.stages):
            self.start(k, step + 1)

    def plan(self):
        planned = []
        last = len(self.stages) - 1
        for k, (begin, *ends) in enumerate(self.times):
            planned.append((begin, 0, k, lambda k=k: self.start(k, 0)))
            for step in range(last + 1):
                when = ends[-1] if step == last else ends[min(step, 4)]
                planned.append((when, 1, k, lambda k=k, step=step: self.end(k, step)))
        return planned


def paced(begins, waits):
    return [[begin + sum(waits[:count]) for count in range(len(waits) + 1)] for begin in begins]


def head_mask(v, half):
    lane = lax.broadcasted_iota(jnp.int32, (1, PAIR), 1)
    keep = (lane < HEAD) if half == 0 else (lane >= HEAD)
    return jnp.where(keep, v, jnp.zeros_like(v))


def attend(qkv, shares, begins, waits, ident, seqs, block=512, per=3):
    rows, width = qkv.shape[0], qkv.shape[1] // 3
    seq_length = rows // seqs
    block = min(block, seq_length)
    pairs = width // PAIR
    count = seq_length // block
    steps = pairs // per
    items = per * count
    wide = per * PAIR

    gathering = Gather([v.shape for v in shares], begins, waits)
    many = len(shares)
    ticks = seqs * steps * items

    def kernel(*refs):
        q_ref, k_ref, v_ref = refs[:3]
        out, total = refs[3 + many : 5 + many]
        v_turned, out_turned, held = refs[5 + 2 * many : 8 + 2 * many]
        gathering.bind(refs[3 : 3 + many], refs[5 + many : 5 + 2 * many], refs[8 + 2 * many :])
        spot = pl.program_id(0) * steps + pl.program_id(1)
        v_turned[...] = jnp.transpose(v_ref[...])

        def place(i):
            pair = i // count
            part = i - pair * count
            return (
                pair,
                pl.ds(pl.multiple_of(pair * PAIR, PAIR), PAIR),
                pl.ds(pl.multiple_of(part * block, block), block),
            )

        def score(i, half):
            _, cols, part = place(i)
            held[half] = mxu(k_ref[:, cols], head_mask(q_ref[part, cols], half), TRANSPOSED)

        def finish(i, half):
            pair, _, part = place(i)
            scores = held[half]
            top = jnp.max(scores, axis=0, keepdims=True)
            exponent = jnp.exp2(scores * SCALE2 - top * SCALE2).astype(BF16)
            head = pl.ds(pl.multiple_of(pair * PAIR + half * HEAD, HEAD), HEAD)
            left = jnp.concatenate([v_turned[head, :], jnp.ones((16, seq_length), BF16)], axis=0)
            mixed = mxu(left, exponent)
            denominator = mixed[HEAD : HEAD + 1]
            out_turned[head, part] = mixed[:HEAD] * (1.0 / denominator)
            total[0, pair, half : half + 1, part] = top * SCALE2 + jnp.log2(denominator)

        score(0, 0)

        def body(i, carry):
            gathering.tick(spot * items + i, ticks)
            score(i, 1)
            finish(i, 0)
            score(jnp.minimum(i + 1, items - 1), 0)
            finish(i, 1)
            return carry

        lax.fori_loop(0, items, body, 0)
        out[...] = jnp.transpose(out_turned[...]).astype(BF16)

        @pl.when(spot == seqs * steps - 1)
        def _():
            gathering.rest(ticks)

    def part_of(which):
        return pl.BlockSpec((seq_length, wide), lambda s, p: (s, which * steps + p))

    return call(
        kernel,
        "attend",
        (seqs, steps),
        [part_of(0), part_of(1), part_of(2)] + gathering.in_specs(),
        [part_of(0), pl.BlockSpec((1, per, 2, seq_length), lambda s, p: (s, p, 0, 0))]
        + gathering.out_specs(),
        [
            jax.ShapeDtypeStruct((rows, width), BF16),
            jax.ShapeDtypeStruct((seqs, pairs, 2, seq_length), F32),
        ]
        + gathering.out_shape(),
        [
            pltpu.VMEM((wide, seq_length), BF16),
            pltpu.VMEM((wide, seq_length), F32),
            pltpu.VMEM((2, seq_length, block), F32),
        ]
        + gathering.scratch(),
        16 * rows * seq_length * width,
        rows * width * 8,
        rows * seq_length * width // HEAD,
        ident,
    )(qkv, qkv, qkv, *shares)


def attend_back(
    qkv, mixture, d_mixture, total, tables, pieces, times, ident, seqs, block=512, per=3
):
    rows, width = mixture.shape
    seq_length = rows // seqs
    block = min(block, seq_length)
    pairs = width // PAIR
    count = seq_length // block
    steps = pairs // per
    items = per * count
    wide = per * PAIR
    exchange = Exchange([v.shape for v in pieces], times)
    many = len(pieces)
    ticks = seqs * steps * items

    def kernel(*refs):
        q_ref, k_ref, v_ref, mix, grad, tot, cos, upp, low = refs[:9]
        dq, dk, dv = refs[9 + many : 12 + many]
        k_turned, dq_turned, dk_sum, dv_sum, inner, s_held, p_held = refs[
            12 + 2 * many : 19 + 2 * many
        ]
        exchange.bind(refs[9 : 9 + many], refs[12 + many : 12 + 2 * many], refs[19 + 2 * many :])
        spot = pl.program_id(0) * steps + pl.program_id(1)
        k_turned[...] = jnp.transpose(k_ref[...])
        product = jnp.transpose(mix[...].astype(F32) * grad[...].astype(F32))
        for pair in range(per):
            for half in range(2):
                lower = pair * PAIR + half * HEAD
                inner[pair, half : half + 1, :] = column_sum(product[lower : lower + HEAD, :])
        dk_sum[...] = jnp.zeros_like(dk_sum)
        dv_sum[...] = jnp.zeros_like(dv_sum)

        def body(i, carry):
            exchange.tick(spot * items + i, ticks)
            pair = i // count
            part = i - pair * count
            cols = pl.ds(pl.multiple_of(pair * PAIR, PAIR), PAIR)
            part = pl.ds(pl.multiple_of(part * block, block), block)
            for half in range(2):
                head = pl.ds(pl.multiple_of(pair * PAIR + half * HEAD, HEAD), HEAD)
                query = head_mask(q_ref[part, cols], half)
                cot = head_mask(grad[part, cols], half)
                s_held[half] = mxu(k_ref[:, cols], query, TRANSPOSED)
                p_held[half] = mxu(v_ref[:, cols], cot, TRANSPOSED)
                probs = jnp.exp2(s_held[half] * SCALE2 - tot[0, pair, half : half + 1, part])
                d_scores = (probs * (p_held[half] - inner[pair, half : half + 1, part])).astype(BF16)
                dv_sum[:, cols] += mxu(probs.astype(BF16), cot)
                dk_sum[:, cols] += mxu(d_scores, query)
                dq_turned[head, part] = mxu(k_turned[head, :], d_scores)
            return carry

        lax.fori_loop(0, items, body, 0)
        d_queries = jnp.transpose(dq_turned[...])
        for source, target in ((d_queries, dq), (dk_sum, dk)):
            for pair in range(per):
                v = source[:, pair * PAIR : (pair + 1) * PAIR] * SCALE
                v = v * cos[...] - from_ahead(v) * upp[...] - from_behind(v) * low[...]
                target[:, pair * PAIR : (pair + 1) * PAIR] = v.astype(BF16)
        dv[...] = dv_sum[...].astype(BF16)

        @pl.when(spot == seqs * steps - 1)
        def _():
            exchange.rest(ticks)

    def part_of(which):
        return pl.BlockSpec((seq_length, wide), lambda s, p: (s, which * steps + p))

    table = whole((seq_length, PAIR))
    grads = jax.ShapeDtypeStruct((rows, width), BF16)
    return call(
        kernel,
        "attend_back",
        (seqs, steps),
        [part_of(0), part_of(1), part_of(2), part_of(0), part_of(0)]
        + [pl.BlockSpec((1, per, 2, seq_length), lambda s, p: (s, p, 0, 0))]
        + [table] * 3
        + exchange.in_specs(),
        [part_of(0), part_of(0), part_of(0)] + exchange.out_specs(),
        [grads, grads, grads] + exchange.out_shape(),
        [
            pltpu.VMEM((wide, seq_length), BF16),
            pltpu.VMEM((wide, seq_length), F32),
            pltpu.VMEM((seq_length, wide), F32),
            pltpu.VMEM((seq_length, wide), F32),
            pltpu.VMEM((per, 2, seq_length), F32),
            pltpu.VMEM((2, seq_length, block), F32),
            pltpu.VMEM((2, seq_length, block), F32),
        ]
        + exchange.scratch(),
        40 * rows * seq_length * width,
        rows * width * 16,
        rows * seq_length * width // HEAD,
        ident,
    )(qkv, qkv, qkv, mixture, d_mixture, total, *tables, *pieces)


def middle_norm(mixture, tokens, span, embed, gain, modulation, weight, seqs, block=512):
    rows, width = tokens.shape
    seq_length = rows // seqs
    block = min(block, seq_length)
    per_seq = seq_length // block

    def kernel(span_ref, mix, tok, emb, gn, mod, w, out):
        step = pl.program_id(0)
        seq = step // per_seq
        first = (step - seq * per_seq) * block
        start, _ = masked_rows(tok[...], emb[...], span_ref[0, seq], span_ref[1, seq], first)
        middle = start + mod[pl.ds(seq, 1), 2 * width : 3 * width] * mxu(mix[...], w[...])
        hat, _ = normalized(middle)
        shift = mod[pl.ds(seq, 1), 3 * width : 4 * width]
        scale = mod[pl.ds(seq, 1), 4 * width : 5 * width]
        out[...] = (hat * (gn[...] * (1.0 + scale)) + shift).astype(BF16)

    row = pl.BlockSpec((block, width), lambda i: (i, 0))
    return call(
        kernel,
        "middle_norm",
        (rows // block,),
        [smem(), row, row, whole((1, width)), whole((1, width)), whole(modulation.shape)]
        + [whole(weight.shape)],
        row,
        jax.ShapeDtypeStruct((rows, width), BF16),
        [],
        2 * rows * width * width,
        rows * width * 6,
    )(span, mixture, tokens, embed, gain, modulation, weight)


def gelu_pair(v):
    root = math.sqrt(2.0 / math.pi)
    square = v * v
    bent = jnp.tanh(v * (root + (root * 0.044715) * square))
    near = 0.5 + 0.5 * bent
    slope = near + (0.5 * v) * (1.0 - bent * bent) * (root + (3.0 * root * 0.044715) * square)
    return v * near, slope


def hidden_units(normed, cot, order, modulation, up, up_bias, down, seqs, block=512):
    rows, width = normed.shape
    units = up.shape[1]
    ways = order.shape[1]
    share, part_units = width // ways, units // ways
    seq_length = rows // seqs
    block = min(block, seq_length)
    per_seq = seq_length // block
    steps = rows // block

    def kernel(order_ref, nrm, g, mod, w_up, b_up, w_down, act, d_up, g_up, g_down, g_bias, d_gate,
               g_sum, n_turned, g_turned, a_held, u_held):
        step = pl.program_id(0)

        @pl.when(step == 0)
        def _():
            g_bias[...] = jnp.zeros_like(g_bias)
            d_gate[...] = jnp.zeros_like(d_gate)
            g_sum[...] = jnp.zeros_like(g_sum)

        @pl.when(step < steps)
        def _():
            seq = step // per_seq
            part = pl.ds(pl.multiple_of(step * block, block), block)
            cotangent = g[...].astype(F32)
            d_branch = (mod[pl.ds(seq, 1), 5 * width : 6 * width] * cotangent).astype(BF16)
            upper = mxu(nrm[...], w_up[...]) + b_up[...]
            active, slope = gelu_pair(upper)
            active = active.astype(BF16)
            d_upper = (mxu(d_branch, w_down[...], TRANSPOSED) * slope).astype(BF16)
            act[...] = active
            a_held[part, :] = active
            d_up[...] = d_upper
            u_held[part, :] = d_upper
            store_shares(n_turned, jnp.transpose(nrm[...]), order_ref, part)
            g_turned[:, part] = jnp.transpose(g[...])
            g_bias[...] += column_sum(d_upper.astype(F32))
            g_sum[pl.ds(seq, 1), :] += column_sum(cotangent)

        @pl.when(step >= steps)
        def _():
            spot = (step - steps) * part_units
            cols = pl.ds(pl.multiple_of(spot, part_units), part_units)
            g_up[...] = mxu(n_turned[...], u_held[:, cols]).astype(BF16).reshape(g_up.shape)
            own = w_down[cols, :].astype(F32)
            total = jnp.zeros((part_units, width), F32)
            for seq in range(seqs):
                lower, upper = seq * seq_length, (seq + 1) * seq_length
                product = mxu(g_turned[:, lower:upper], a_held[lower:upper, cols])
                product = jnp.transpose(product)
                total += product * mod[seq : seq + 1, 5 * width : 6 * width]
                d_gate[seq : seq + 1, :] += column_sum(product * own)
            g_down[0] = total.astype(BF16)

    def early(i, *_):
        return (jnp.minimum(i, steps - 1), 0)

    def late(i):
        return jnp.maximum(i - steps, 0)

    def fixed(shape):
        return pl.BlockSpec(shape, lambda *_: (0,) * len(shape))

    return pl.pallas_call(
        kernel,
        name="hidden_units",
        grid_spec=pltpu.PrefetchScalarGridSpec(
            num_scalar_prefetch=1,
            grid=(steps + ways,),
            in_specs=[
                pl.BlockSpec((block, width), early),
                pl.BlockSpec((block, width), early),
                whole(modulation.shape),
                whole(up.shape),
                whole(up_bias.shape),
                whole(down.shape),
            ],
            out_specs=(
                pl.BlockSpec((block, units), early),
                pl.BlockSpec((block, units), early),
                pl.BlockSpec((ways, share, part_units), lambda i, _: (0, 0, late(i))),
                pl.BlockSpec((1, part_units, width), lambda i, o: (o[1, late(i)], 0, 0)),
                fixed((1, units)),
                fixed((seqs, width)),
                fixed((seqs, width)),
            ),
            scratch_shapes=[
                pltpu.VMEM((width, rows), BF16),
                pltpu.VMEM((width, rows), BF16),
                pltpu.VMEM((rows, units), BF16),
                pltpu.VMEM((rows, units), BF16),
            ],
        ),
        out_shape=(
            jax.ShapeDtypeStruct((rows, units), BF16),
            jax.ShapeDtypeStruct((rows, units), BF16),
            jax.ShapeDtypeStruct((ways, share, units), BF16),
            jax.ShapeDtypeStruct((ways, part_units, width), BF16),
            jax.ShapeDtypeStruct((1, units), F32),
            jax.ShapeDtypeStruct((seqs, width), F32),
            jax.ShapeDtypeStruct((seqs, width), F32),
        ),
        compiler_params=pltpu.CompilerParams(vmem_limit_bytes=VMEM_BYTES),
        cost_estimate=pl.CostEstimate(
            flops=8 * rows * width * units,
            bytes_accessed=rows * (width * 4 + units * 4) + 8 * width * units,
            transcendentals=rows * units,
        ),
    )(order, normed, cot, modulation, up, up_bias, down)


def middle_back(
    mixture, tokens, cot, span, embed, gain, modulation, out_weight, d_uppers, ups, pieces, times,
    ident, seqs, ways, block=256,
):
    rows, width = tokens.shape
    seq_length = rows // seqs
    block = min(block, seq_length)
    per_seq = seq_length // block
    steps = rows // block
    groups = len(d_uppers)
    units = d_uppers[0].shape[1]
    share = width // ways
    exchange = Exchange([v.shape for v in pieces], times)
    many = len(pieces)

    def kernel(*refs):
        span_ref, mix, tok, g, emb, gn, mod, w_out = refs[:8]
        d_ups, w_ups = refs[8 : 8 + groups], refs[8 + groups : 8 + 2 * groups]
        spot = 8 + 2 * groups
        ins, spot = refs[spot : spot + many], spot + many
        d_middle_out, d_mix, g_out, sums = refs[spot : spot + 4]
        outs, spot = refs[spot + 4 : spot + 4 + many], spot + 4 + many
        g_sum = refs[spot]
        exchange.bind(ins, outs, refs[spot + 1 :])
        step = pl.program_id(0)
        seq = step // per_seq
        first = (step - seq * per_seq) * block
        exchange.tick(step, steps)

        @pl.when(step == 0)
        def _():
            g_sum[...] = jnp.zeros_like(g_sum)

        @pl.when(step == seq * per_seq)
        def _():
            sums[...] = jnp.zeros_like(sums)

        def vector(which):
            return mod[pl.ds(seq, 1), which * width : (which + 1) * width]

        attended = mxu(mix[...], w_out[...])
        start, _ = masked_rows(tok[...], emb[...], span_ref[0, seq], span_ref[1, seq], first)
        hat, inverse = normalized(start + vector(2) * attended)
        d_normed = mxu(d_ups[0][...], w_ups[0][...], TRANSPOSED)
        for group in range(1, groups):
            d_normed += mxu(d_ups[group][...], w_ups[group][...], TRANSPOSED)
        d_middle = g[...].astype(F32) + norm_back(
            d_normed * (gn[...] * (1.0 + vector(4))), hat, inverse
        )
        d_middle_out[...] = d_middle
        d_attended = (vector(2) * d_middle).astype(BF16)
        d_mix[...] = mxu(d_attended, w_out[...], TRANSPOSED).astype(BF16)
        g_sum[...] += mxu(jnp.transpose(mix[...]), d_attended)
        sums[0, 0:1, :] += column_sum(d_normed)
        sums[0, 1:2, :] += column_sum(d_normed * hat)
        sums[0, 2:3, :] += column_sum(d_middle * attended)

        @pl.when(step == steps - 1)
        def _():
            me = exchange.at["narrow"]
            for position, owner in enumerate((flip(flip(me, 1), 2), flip(me, 1), flip(me, 2), me)):
                spot = pl.ds(pl.multiple_of(owner * share, share), share)
                g_out[position] = g_sum[spot, :].astype(BF16)
            exchange.rest(steps)

    row = pl.BlockSpec((block, width), lambda i: (i, 0))
    unit_row = pl.BlockSpec((block, units), lambda i: (i, 0))
    return call(
        kernel,
        "middle_back",
        (steps,),
        [smem(), row, row, row, whole((1, width)), whole((1, width)), whole(modulation.shape)]
        + [whole(out_weight.shape)]
        + [unit_row] * groups
        + [whole(ups[0].shape)] * groups
        + exchange.in_specs(),
        [
            row,
            row,
            pl.BlockSpec((ways, share, width), lambda i: (0, 0, 0)),
            pl.BlockSpec((1, 8, width), lambda i: (i // per_seq, 0, 0)),
        ]
        + exchange.out_specs(),
        [
            jax.ShapeDtypeStruct((rows, width), F32),
            jax.ShapeDtypeStruct((rows, width), BF16),
            jax.ShapeDtypeStruct((ways, share, width), BF16),
            jax.ShapeDtypeStruct((seqs, 8, width), F32),
        ]
        + exchange.out_shape(),
        [pltpu.VMEM((width, width), F32)] + exchange.scratch(),
        rows * width * (2 * units * groups + 6 * width),
        rows * (width * 12 + units * groups * 2) + 2 * width * units * groups,
        0,
        ident,
    )(
        span, mixture, tokens, cot, embed, gain, modulation, out_weight, *d_uppers, *ups, *pieces
    )


class Finale(Steps):
    def __init__(self, ways):
        self.ways = ways
        self.wide = lax.axis_size("wide")

    def scratch(self, columns):
        dma = pltpu.SemaphoreType.DMA
        return [
            pltpu.VMEM((self.ways, 8, columns), F32),
            pltpu.VMEM((self.ways, 8, columns), F32),
            pltpu.VMEM((self.wide, 8, columns), F32),
            dma((self.ways,)),
            dma((self.ways,)),
            dma((self.wide,)),
            dma((self.wide,)),
        ]

    def bind(self, held):
        self.parts, self.narrow_got, self.wide_got, *self.sems = held
        self.locate()

    def others(self):
        targets = []
        for offset in range(1, self.ways):
            targets.append({"narrow": lax.rem(self.at["narrow"] + offset, self.ways)})
        for offset in range(1, self.wide):
            targets.append({"wide": lax.rem(self.at["wide"] + offset, self.wide)})
        return targets

    def greet(self):
        barrier = pltpu.get_barrier_semaphore()
        targets = self.others()
        for target in targets:
            pl.semaphore_signal(
                barrier, inc=1, device_id=target, device_id_type=pl.DeviceIdType.MESH
            )
        pl.semaphore_wait(barrier, len(targets))

    def along_narrow(self, offset):
        target = lax.rem(self.at["narrow"] + offset, self.ways)
        return pltpu.make_async_remote_copy(
            src_ref=self.parts.at[target],
            dst_ref=self.narrow_got.at[self.at["narrow"]],
            send_sem=self.sems[0].at[offset],
            recv_sem=self.sems[1].at[offset],
            device_id={"narrow": target},
            device_id_type=pl.DeviceIdType.MESH,
        )

    def along_wide(self, offset):
        me = self.at["wide"]
        return pltpu.make_async_remote_copy(
            src_ref=self.wide_got.at[me],
            dst_ref=self.wide_got.at[me],
            send_sem=self.sems[2].at[offset],
            recv_sem=self.sems[3].at[offset],
            device_id={"wide": lax.rem(me + offset, self.wide)},
            device_id_type=pl.DeviceIdType.MESH,
        )

    def begin(self):
        for offset in range(1, self.ways):
            self.along_narrow(offset).start()
        me = self.at["narrow"]
        self.narrow_got[pl.ds(me, 1)] = self.parts[pl.ds(me, 1)]

    def spread(self, seqs, row_lanes):
        for offset in range(1, self.ways):
            self.along_narrow(offset).wait()
        me = self.at["wide"]
        for way in range(self.ways):
            self.wide_got[pl.ds(me, 1), way * seqs : (way + 1) * seqs, 0:row_lanes] = (
                self.narrow_got[way : way + 1, 0:seqs, 0:row_lanes]
            )
        total = self.narrow_got[0:1, :, row_lanes:]
        for way in range(1, self.ways):
            total += self.narrow_got[way : way + 1, :, row_lanes:]
        self.wide_got[pl.ds(me, 1), :, row_lanes:] = total
        for offset in range(1, self.wide):
            self.along_wide(offset).start()

    def close(self):
        for offset in range(1, self.wide):
            self.along_wide(offset).wait()


def finish(
    turned, d_parts, tokens, cot, d_middle, mixture, span, embed, gain, modulation, weights,
    out_weight, down_bias, actives, downs, features, rows_two, vectors_two, times, ident, seqs,
    tile=256, block=512, late_block=256,
):
    rows, width = tokens.shape
    ways = lax.axis_size("narrow")
    share = width // ways
    seq_length = rows // seqs
    block, late_block = min(block, seq_length), min(late_block, seq_length)
    per_seq, late_per_seq = seq_length // block, seq_length // late_block
    tiles = width // tile
    columns, group_units = modulation.shape[1] // ways, actives[0].shape[1]
    groups = len(actives)
    time_width = features.shape[1]
    window = 2 * PAIR
    lanes = columns + time_width + window
    early, middle, late = 3 * tiles, rows // block, rows // late_block
    steps = early + middle + late
    exchange = Exchange([(ways, share, width)] * 3, times)
    finale = Finale(ways)

    def kernel(*refs):
        (
            span_ref, left, c_q, c_k, c_v, tok, d_mid, r_q, r_k, r_v, emb, gn, mod, w_q, w_k, w_v,
            tok_late, mix, w_out, b_down, feat, two, vec,
        ) = refs[:23]
        acts, w_downs = refs[23 : 23 + groups], refs[23 + groups : 23 + 2 * groups]
        spot = 23 + 2 * groups
        g_tok, block_out, g_ada, g_ada_bias, g_vec = refs[spot : spot + 5]
        outs = refs[spot + 5 : spot + 8]
        grads, sums = refs[spot + 8 : spot + 10]
        small = 7
        exchange.bind(
            [grads.at[part] for part in range(3)], outs, refs[spot + 10 + small :]
        )
        finale.bind(refs[spot + 10 : spot + 10 + small])
        step = pl.program_id(0)

        @pl.when(step == 0)
        def _():
            finale.greet()
            sums[...] = jnp.zeros_like(sums)

        exchange.tick(step, steps)

        for part, source in enumerate((c_q, c_k, c_v)):

            @pl.when((step >= part * tiles) & (step < (part + 1) * tiles))
            def _(part=part, source=source):
                cols = pl.ds(pl.multiple_of((step - part * tiles) * tile, tile), tile)
                product = mxu(left[...], source[...]).astype(BF16)
                grads[part, :, :, cols] = product.reshape(ways, share, tile)

        @pl.when((step >= early) & (step < early + middle))
        def _():
            at = step - early
            seq = at // per_seq
            first = (at - seq * per_seq) * block
            start, inside = masked_rows(
                tok[...], emb[...], span_ref[0, seq], span_ref[1, seq], first
            )
            hat, inverse = normalized(start)
            d_normed = mxu(r_q[...], w_q[...], TRANSPOSED)
            d_normed += mxu(r_k[...], w_k[...], TRANSPOSED)
            d_normed += mxu(r_v[...], w_v[...], TRANSPOSED)
            scale = mod[pl.ds(seq, 1), width : 2 * width]
            d_start = d_mid[...] + norm_back(d_normed * (gn[...] * (1.0 + scale)), hat, inverse)
            g_tok[...] = jnp.where(inside, 0.0, d_start)
            sums[seq, 0:1, :] += column_sum(d_normed)
            sums[seq, 1:2, :] += column_sum(d_normed * hat)
            sums[seq, 2:3, :] += column_sum(jnp.where(inside, d_start, 0.0))

        @pl.when(step == early + middle)
        def _():
            parts = finale.parts
            embed_sum = jnp.zeros((1, width), F32)
            gain_sum = jnp.zeros((1, width), F32)
            for seq in range(seqs):
                shift, scale = sums[seq, 0:1, :], sums[seq, 1:2, :]
                gain_sum += scale * (1.0 + mod[seq : seq + 1, width : 2 * width])
                embed_sum += sums[seq, 2:3, :]
                row = jnp.concatenate([shift, scale * gn[...], two[seq : seq + 1, :]], axis=1)
                for way in range(ways):
                    parts[way, seq : seq + 1, 0:columns] = row[
                        :, way * columns : (way + 1) * columns
                    ]
            for way in range(ways):
                parts[way, 0:seqs, columns : columns + time_width] = feat[...]
                lower = PAIR * (share * way // PAIR)
                parts[way, 0:1, columns + time_width :] = embed_sum[:, lower : lower + window]
                parts[way, 1:2, columns + time_width :] = gain_sum[:, lower : lower + window]
                parts[way, 2:8, columns + time_width :] = vec[way, 2:8, :]
            finale.begin()

        @pl.when(step == early + middle + 2)
        def _():
            finale.spread(seqs, columns + time_width)

        @pl.when(step >= early + middle)
        def _():
            at = step - early - middle
            seq = at // late_per_seq
            first = (at - seq * late_per_seq) * late_block
            start, _ = masked_rows(
                tok_late[...], emb[...], span_ref[0, seq], span_ref[1, seq], first
            )
            attended = mxu(mix[...], w_out[...])
            branch = mxu(acts[0][...], w_downs[0][...])
            for group in range(1, groups):
                branch += mxu(acts[group][...], w_downs[group][...])
            branch += b_down[...]
            hidden = start + mod[pl.ds(seq, 1), 2 * width : 3 * width] * attended
            block_out[...] = (
                hidden + mod[pl.ds(seq, 1), 5 * width : 6 * width] * branch
            ).astype(BF16)

        @pl.when(step == steps - 1)
        def _():
            finale.close()
            got = finale.wide_got
            every = got[...].reshape(finale.wide * 8, lanes)
            d_mods, feats = every[:, 0:columns], every[:, columns : columns + time_width]
            g_ada[...] = lax.dot_general(
                jnp.transpose(feats), d_mods, PLAIN, precision=FULL_PRECISION,
                preferred_element_type=F32,
            )
            g_ada_bias[...] = column_sum(d_mods)
            total = got[0, :, columns + time_width :]
            for index in range(1, finale.wide):
                total += got[index, :, columns + time_width :]
            g_vec[...] = total
            exchange.rest(steps)

    def column(part):
        return pl.BlockSpec((rows, tile), lambda i: (0, jnp.clip(i - part * tiles, 0, tiles - 1)))

    row = pl.BlockSpec((block, width), lambda i: (jnp.clip(i - early, 0, middle - 1), 0))

    def late_row(wide):
        return pl.BlockSpec(
            (late_block, wide), lambda i: (jnp.maximum(i - early - middle, 0), 0)
        )

    def fixed(shape):
        return pl.BlockSpec(shape, lambda i: (0,) * len(shape))

    return call(
        kernel,
        "finish",
        (steps,),
        [smem(), whole(turned.shape), column(0), column(1), column(2), row, row, row, row, row]
        + [whole((1, width)), whole((1, width)), whole(modulation.shape)]
        + [whole((width, width))] * 3
        + [late_row(width), late_row(width), whole((width, width)), whole((1, width))]
        + [whole(features.shape), whole(rows_two.shape), whole(vectors_two.shape)]
        + [late_row(group_units)] * groups
        + [whole((group_units, width))] * groups,
        [
            row,
            late_row(width),
            fixed((time_width, columns)),
            fixed((1, columns)),
            fixed((8, window)),
        ]
        + exchange.out_specs(),
        [
            jax.ShapeDtypeStruct((rows, width), F32),
            jax.ShapeDtypeStruct((rows, width), BF16),
            jax.ShapeDtypeStruct((time_width, columns), F32),
            jax.ShapeDtypeStruct((1, columns), F32),
            jax.ShapeDtypeStruct((8, window), F32),
        ]
        + exchange.out_shape(),
        [pltpu.VMEM((3, ways, share, width), BF16), pltpu.VMEM((seqs, 8, width), F32)]
        + finale.scratch(lanes)
        + exchange.scratch(),
        2 * rows * width * (7 * width + group_units * groups),
        rows * (width * 24 + 2 * group_units * groups),
        0,
        ident,
    )(
        span, turned, *d_parts, tokens, d_middle, *d_parts, embed, gain, modulation, *weights,
        tokens, mixture, out_weight, down_bias, features, rows_two, vectors_two, *actives, *downs,
    )


def gather_first(small, ada, weight, ident):
    share, wide = weight.shape
    width = wide // 3
    shapes = [small.shape, ada.shape] + [(share, width)] * 3
    gathering = Gather(shapes, [0] * 5, [0] * 3)

    def kernel(*refs):
        ins = [refs[0], refs[1]] + [refs[2].at[:, k * width : (k + 1) * width] for k in range(3)]
        gathering.bind(ins, refs[3:8], refs[8:])
        gathering.greet()
        gathering.begin(0)
        gathering.begin(1)
        gathering.begin(2)
        for k in range(5):
            gathering.relay(k)
            if k + 3 < 5:
                gathering.begin(k + 3)
            if k > 0:
                gathering.share(k - 1)
        gathering.share(4)
        for k in range(5):
            gathering.close(k)

    return call(
        kernel,
        "gather_first",
        (),
        [pl.BlockSpec(memory_space=pl.ANY)] * 3,
        gathering.out_specs(),
        gathering.out_shape(),
        gathering.scratch(),
        0,
        8 * share * wide,
        0,
        ident,
    )(small, ada, weight)


def per_device(
    tokens,
    timestep,
    span_start,
    span_length,
    mask_embed,
    ada_weight,
    ada_bias,
    norm_first,
    query_key_value_weight,
    output_weight,
    norm_second,
    up_projection_weight,
    up_projection_bias,
    down_projection_weight,
    down_projection_bias,
    cotangent,
):
    seqs = timestep.shape[0]
    rows, width = tokens.shape
    seq_length = rows // seqs
    ways = lax.axis_size("narrow")
    me = lax.axis_index("narrow")
    share = width // ways
    unit_share = down_projection_weight.shape[0]
    part = unit_share // GROUPS
    units = ways * part
    time_width, columns = ada_weight.shape

    vectors = (
        ada_bias, mask_embed, norm_first, norm_second, down_projection_bias, up_projection_bias,
    )
    small = jnp.stack([jnp.pad(v, (0, columns - v.shape[0])) for v in vectors])
    small = jnp.pad(small, ((0, 32 - len(vectors)), (0, 0)))
    small, ada, w_q, w_k, w_v = gather_first(small, ada_weight, query_key_value_weight, 0)
    up_parts = up_projection_weight.reshape(share, ways, GROUPS, part)
    shares = [output_weight]
    for group in range(GROUPS):
        shares.append(up_parts[:, :, group].reshape(share, units))
        shares.append(down_projection_weight[group * part : (group + 1) * part])

    small = small.reshape(ways, 32, columns)[:, : len(vectors)].astype(F32)
    bias_ada, embed, gain_one, gain_two, bias_down, bias_up = [
        small[:, index, : v.shape[0]].reshape(1, -1) for index, v in enumerate(vectors)
    ]
    ada = jnp.moveaxis(ada.reshape(ways, time_width, columns), 0, 1).reshape(time_width, -1)
    features = time_features(timestep, time_width)
    modulation = jnp.dot(features, ada.astype(F32), precision=FULL_PRECISION) + bias_ada
    span = jnp.stack([span_start, span_length])
    tables = rotary_tables(seq_length)
    places = jnp.arange(ways)
    order = jnp.stack(
        [
            me ^ (2 * (1 - places % 2) + (1 - places // 2)),
            2 * (1 - (me ^ places) % 2) + (1 - (me ^ places) // 2),
        ]
    ).astype(jnp.int32)

    qkv, turned_one = project(
        tokens, span, order, embed, gain_one, modulation, (w_q, w_k, w_v), tables, seqs
    )
    mixture, total, w_out, *rest = attend(
        qkv, shares, [0, 1, 4, 7, 10, 13, 16], [4, 4, 3], 1, seqs
    )
    ups, downs = rest[0::2], rest[1::2]
    normed_two = middle_norm(mixture, tokens, span, embed, gain_two, modulation, w_out, seqs)
    bias_parts = bias_up.reshape(ways, GROUPS, part)
    actives, d_uppers, pieces, g_biases, d_gate_two = [], [], [], [], 0.0
    for group in range(GROUPS):
        active, d_upper, g_up, g_down, g_bias, d_gate, g_sum = hidden_units(
            normed_two,
            cotangent,
            order,
            modulation,
            ups[group],
            bias_parts[:, group].reshape(1, units),
            downs[group],
            seqs,
        )
        actives.append(active)
        d_uppers.append(d_upper)
        pieces += [g_up, g_down]
        g_biases.append(g_bias)
        d_gate_two += d_gate
    d_gate_two += bias_down * g_sum
    d_middle, d_mixture, g_out, sums_two, *done_first = middle_back(
        mixture, tokens, cotangent, span, embed, gain_two, modulation, w_out, d_uppers, ups,
        pieces[:2], paced([0, 1], [1, 2, 1, 1, 2, 1]), 2, seqs, ways,
    )
    d_q, d_k, d_v, *done_second = attend_back(
        qkv, mixture, d_mixture, total, tables, pieces[2:] + [g_out],
        paced([0, 2, 4, 6, 8], [1, 5, 3, 3, 5, 3]), 3, seqs,
    )
    scale_two = modulation[:, 4 * width : 5 * width]
    rows_two = jnp.concatenate(
        [sums_two[:, 2], sums_two[:, 0], sums_two[:, 1] * gain_two, d_gate_two], axis=1
    )
    g_norm_two = jnp.sum(sums_two[:, 1] * (1.0 + scale_two), axis=0)
    g_bias_down = jnp.sum(modulation[:, 5 * width :] * g_sum, axis=0)
    lowers = [PAIR * (share * way // PAIR) for way in range(ways)]
    vectors_two = jnp.stack(
        [
            jnp.stack([v[lower : lower + 2 * PAIR] for lower in lowers])
            for v in (g_norm_two, g_norm_two, g_norm_two, g_bias_down)
        ]
        + [v.reshape(ways, part) for v in g_biases]
        + [jnp.zeros((ways, 2 * PAIR), F32)],
        axis=1,
    )
    grad_tokens, block_out, grad_ada_weight, grad_ada_bias, vectors, *g_qkv = finish(
        turned_one, (d_q, d_k, d_v), tokens, cotangent, d_middle, mixture, span, embed, gain_one,
        modulation, (w_q, w_k, w_v), w_out, bias_down, actives, downs, features, rows_two,
        vectors_two,
        [[3, 5, 11, 12, 13, 16, 18], [6, 8, 12, 13, 15, 18, 20], [9, 10, 14, 16, 18, 20, 21]],
        4, seqs,
    )
    skip = lax.rem(share * me, PAIR)
    own = lax.dynamic_slice_in_dim(vectors[:4], skip, share, 1)
    g_ups, g_downs = zip(*[done_first] + [done_second[2 * k : 2 * k + 2] for k in range(2)])
    grad_up = jnp.stack([v.reshape(share, ways, part) for v in g_ups], axis=2)
    return (
        block_out,
        grad_tokens,
        own[0],
        grad_ada_weight,
        grad_ada_bias[0],
        own[1],
        jnp.concatenate(g_qkv, axis=1).astype(F32),
        done_second[4].astype(F32),
        own[2],
        grad_up.reshape(share, ways * unit_share).astype(F32),
        vectors[4 : 4 + GROUPS].reshape(-1),
        jnp.concatenate(g_downs).astype(F32),
        own[3],
    )


def solution(mesh):
    rows = P(("wide", "narrow"), None)
    per_seq = P(("wide", "narrow"))
    vector, matrix, columns = P("narrow"), P("narrow", None), P(None, "narrow")
    return jax.shard_map(
        per_device,
        mesh=mesh,
        in_specs=(
            rows, per_seq, per_seq, per_seq, vector, columns, vector, vector,
            matrix, matrix, vector, matrix, vector, matrix, vector, rows,
        ),
        out_specs=(
            rows, rows, vector, columns, vector, vector, matrix, matrix, vector, matrix,
            vector, matrix, vector,
        ),
        check_vma=False,
    )
```

time: 681 us -> 528 us (0.78)
  waiting for transfers between devices: 183 us -> 0 us
  Pallas kernels: 289 us -> 454 us
  blocking collectives: 117 us -> 0 us
  between operations: 15.2 us -> 1.45 us
    pallas_call x7, Pallas kernels: 162 us -> 259 us  [the longest x1 73.4 us: finish(): call(kernel, 'finish', (steps,), [smem(), whole(turned.shape), column(0),...]
    reduce_scatter x8 -> x0, waiting for transfers between devices: 78.9 us -> none  [reduce_share(): lax.psum_scatter(v, 'narrow', scatter_dimension=0, tiled=True)]
    all_gather x9 -> x0, waiting for transfers between devices: 70.3 us -> none  [gather(): return lax.all_gather(v, 'narrow', axis=axis, tiled=True)]
    pallas_call x1, Pallas kernels: 37.4 us -> 87.2 us  [attend(): call(kernel, 'attend', (seqs, steps), [part_of(0), part_of(1), part_of(2)...]
    unnamed x1 -> x0, blocking collectives: 42.9 us -> none
    psum x1 -> x0, blocking collectives: 41.9 us -> none  [per_device(): vectors = lax.psum(vectors, ('wide', 'narrow'))]
    all_gather x1 -> x0, blocking collectives: 32 us -> none  [per_device(): d_modulation = lax.all_gather(d_modulation, 'wide', axis=0, tiled=True)]
    psum x1 -> x0, waiting for transfers between devices: 29.6 us -> none  [reduce_share(): lax.psum(lax.psum_scatter(v, 'narrow', scatter_dimension=0, tiled=True),...]
  transfers between devices with their start and end apart: 19 -> 0, of which waited for: 9 -> 0; matrix products, arithmetic and copies ran while one was open for 7% -> 0% of each run, Pallas kernels for 43% -> 0%
where the time goes in v2:
time: 528 us; the launch traced here: 519 us
  Pallas kernels  454 us (86%)
  local copies, waits for them, and re-layouts  42.1 us (8%)
  other arithmetic  19.5 us (4%)
    pallas_call x1, Pallas kernels, attend_back(): call(kernel, 'attend_back', (seqs, steps), [part_of(0), part_of(1), part_...  99.6 us
    pallas_call x1, Pallas kernels, attend(): call(kernel, 'attend', (seqs, steps), [part_of(0), part_of(1), part_of(2)...  87.2 us
    pallas_call x1, Pallas kernels, finish(): call(kernel, 'finish', (steps,), [smem(), whole(turned.shape), column(0),...  73.4 us
    pallas_call x3, Pallas kernels, hidden_units(): pl.pallas_call(kernel, name='hidden_units', grid_spec=pltpu.PrefetchScala...  70.4 us
    pallas_call x1, Pallas kernels, middle_back(): call(kernel, 'middle_back', (steps,), [smem(), row, row, row, whole((1, w...  57.8 us
    pallas_call x1, Pallas kernels, gather_first(): call(kernel, 'gather_first', (), [pl.BlockSpec(memory_space=pl.ANY)] * 3,...  42.5 us
    pallas_call x1, Pallas kernels, project(): call(kernel, 'project', (rows // block,), [smem(), smem(), pl.BlockSpec((...  14.9 us
    unnamed x52, local copies, waits for them, and re-layouts  12.7 us

profile of v2, /device:TPU:0, one launch (start us, length us, event | category | flops | bytes accessed | tf_op | source)
XLA Modules:
  0.0 518.8 jit_solution(6873485508495579480)
XLA Ops:
  7.3 42.5 %gather_first.1 = (bf16[128,1152]{1,0:T(8,128)(2,1)}, bf16[512,1152]{1,0:T(8,128)(2,1)}, bf16[768,768]{1,0:T(8,128)(2,1)}, bf16[768,768]{1,0:T(8,128)(2,1)}, bf16[768,768]{1,0:T(8,128)(2,1)}) custom-call(bf16[32,1152]{1,0:T(8,128)(2,1)} %pad.26.refs_0_, bf16[128,1152]{1,0:T(8,128)(2,1)} %refs_1_.1, bf16[192,2304]{1,0:T(8,128)(2,1)} %refs_2_.2), custom_call_target="tpu_custom_call" | custom-call | bytes 3538944 | tf_op jit(solution)/shard_map/gather_first/pallas_call | solution.py:1152
  52.9 1.7 copy.49
  54.6 1.6 convolution_add_fusion.mod.refs_6_.refs_12_
  56.3 2.0 fusion
  58.3 2.4 pad_maximum_fusion.2
  60.7 14.9 %project.1 = (bf16[2048,2304]{1,0:T(8,128)(2,1)}, bf16[768,2048]{1,0:T(8,128)(2,1)}) custom-call(s32[2,2]{1,0:T(2,128)} %pad_add_fusion.span_ref.refs_0_, s32[2,4]{1,0:T(2,128)} %pad_add_fusion.1.order_ref, bf16[2048,768]{1,0:T(8,128)(2,1)} %refs_16_.1, f32[1,768]{1,0:T(1,128)} %reshape_squeeze.31.emb.refs_4_.refs_10_, ...), custom_call_target="tpu_custom_call" | custom-call | flops 7247757312 | bytes 19267584 | tf_op jit(solution)/shard_map/project/pallas_call | solution.py:142
  75.6 1.7 reshape.208
  77.4 5.4 %slice_reduce_fusion = (bf16[192,4,256]{2,1,0:T(4,128)(2,1)S(1)}, bf16[192,4,256]{2,1,0:T(4,128)(2,1)S(1)}, bf16[192,4,256]{2,1,0:T(4,128)(2,1)S(1)}) fusion(bf16[192,4,3,256]{3,2,1,0:T(4,128)(2,1)S(1)} %reshape.208), kind=kLoop, calls=%fused_computation.4 | loop fusion | bytes 2359296 | tf_op jit(solution)/shard_map/slice | solution.py:1205
  86.3 87.2 %attend.1 = (bf16[2048,768]{1,0:T(8,128)(2,1)}, f32[2,6,2,1024]{3,2,1,0:T(2,128)}, bf16[768,768]{1,0:T(8,128)(2,1)}, bf16[768,1024]{1,0:T(8,128)(2,1)}, bf16[102...) custom-call(bf16[2048,2304]{1,0:T(8,128)(2,1)} %get-tuple-element.76, ...), custom_call_target="tpu_custom_call" | custom-call | flops 25769803776 | bytes 12582912 | tf_op jit(solution)/shard_map/attend/pallas_call | solution.py:483
  174.2 8.2 %middle_norm.1.nrm = bf16[2048,768]{1,0:T(8,128)(2,1)} custom-call(s32[2,2]{1,0:T(2,128)} %pad_add_fusion.span_ref.refs_0_, bf16[2048,768]{1,0:T(8,128)(2,1)} %get-tuple-element.77.mix.refs_1_.refs_3_.refs_17_, bf16[2048,768]{1,0:T(8,128)(2,1)} %refs_16_.1, f32[1,768]{1,0:T(1,128)} %reshape_squeeze.31.emb.refs_4_.refs_10_, ...), custom_call_target="tpu_custom_call" | custom-call | flops 2415919104 | bytes 9437184 | tf_op jit(solution)/shard_map/middle_norm/pallas_call | solution.py:622
  183.0 23.4 %hidden_units.3 = (bf16[2048,1024]{1,0:T(8,128)(2,1)}, bf16[2048,1024]{1,0:T(8,128)(2,1)}, bf16[4,192,1024]{2,1,0:T(8,128)(2,1)}, bf16[4,256,768]{2,1,0:T(8,128)...) custom-call(s32[2,4]{1,0:T(2,128)} %pad_add_fusion.1.order_ref, bf16[2048,768]{1,0:T(8,128)(2,1)} %middle_norm.1.nrm, ...), custom_call_target="tpu_custom_call" | custom-call | flops 12884901888 | bytes 20971520 | tf_op jit(solution)/shard_map/hidden_units/pallas_call | solution.py:708
  207.0 23.4 %hidden_units.4 = (bf16[2048,1024]{1,0:T(8,128)(2,1)}, bf16[2048,1024]{1,0:T(8,128)(2,1)}, bf16[4,192,1024]{2,1,0:T(8,128)(2,1)}, bf16[4,256,768]{2,1,0:T(8,128)...) custom-call(s32[2,4]{1,0:T(2,128)} %pad_add_fusion.1.order_ref, bf16[2048,768]{1,0:T(8,128)(2,1)} %middle_norm.1.nrm, ...), custom_call_target="tpu_custom_call" | custom-call | flops 12884901888 | bytes 20971520 | tf_op jit(solution)/shard_map/hidden_units/pallas_call | solution.py:708
  231.0 23.6 %hidden_units.5 = (bf16[2048,1024]{1,0:T(8,128)(2,1)}, bf16[2048,1024]{1,0:T(8,128)(2,1)}, bf16[4,192,1024]{2,1,0:T(8,128)(2,1)}, bf16[4,256,768]{2,1,0:T(8,128)...) custom-call(s32[2,4]{1,0:T(2,128)} %pad_add_fusion.1.order_ref, bf16[2048,768]{1,0:T(8,128)(2,1)} %middle_norm.1.nrm, ...), custom_call_target="tpu_custom_call" | custom-call | flops 12884901888 | bytes 20971520 | tf_op jit(solution)/shard_map/hidden_units/pallas_call | solution.py:708
  254.6 57.8 %middle_back.1 = (f32[2048,768]{1,0:T(8,128)}, bf16[2048,768]{1,0:T(8,128)(2,1)}, bf16[4,192,768]{2,1,0:T(8,128)(2,1)}, f32[2,8,768]{2,1,0:T(8,128)}, bf16[192,1...) custom-call(s32[2,2]{1,0:T(2,128)} %pad_add_fusion.span_ref.refs_0_, ...), custom_call_target="tpu_custom_call" | custom-call | flops 16911433728 | bytes 36175872 | tf_op jit(solution)/shard_map/middle_back/pallas_call | solution.py:823
  312.4 99.6 %attend_back.1 = (bf16[2048,768]{1,0:T(8,128)(2,1)}, bf16[2048,768]{1,0:T(8,128)(2,1)}, bf16[2048,768]{1,0:T(8,128)(2,1)}, bf16[192,1024]{1,0:T(8,128)(2,1)}, bf...) custom-call(bf16[2048,2304]{1,0:T(8,128)(2,1)} %get-tuple-element.76.re, ...), custom_call_target="tpu_custom_call" | custom-call | flops 64424509440 | bytes 25165824 | tf_op jit(solution)/shard_map/attend_back/pallas_call | solution.py:577
  415.1 73.4 %finish.1 = (f32[2048,768]{1,0:T(8,128)}, bf16[2048,768]{1,0:T(8,128)(2,1)}, f32[128,1152]{1,0:T(8,128)}, f32[1,1152]{1,0:T(1,128)}, f32[8,256]{1,0:T(8,128)}, /...) custom-call(s32[2,2]{1,0:T(2,128)} %pad_add_fusion.span_ref.refs_0_, ...), custom_call_target="tpu_custom_call" | custom-call | flops 26575110144 | bytes 50331648 | tf_op jit(solution)/shard_map/finish/pallas_call | solution.py:1089
  491.2 2.5 maximum_convert_fusion.2
  494.6 1.6 stack_reshape.26
  496.2 1.6 stack_reshape.25
  499.4 4.1 maximum_convert_fusion
  503.6 2.9 reshape.210
  507.0 2.8 maximum_convert_fusion.1
  509.9 1.7 copy.67
  511.5 6.0 %copy.68 = f32[2048,768]{1,0:T(8,128)} copy(f32[2048,768]{1,0:T(8,128)} %get-tuple-element.182) | data formatting | bytes 12582912
  (104 shorter events, 25.2 us)
Async XLA Ops:
  0.6 52.0 %copy-start.20 = (s32[2]{0:T(128)S(1)}, s32[2]{0:T(128)}, u32[]{:S(2)}) copy-start(s32[2]{0:T(128)} %param.17) | copy-start | bytes 28
  52.9 3.4 copy-start.19
  60.7 15.0 %copy-start.2 = (bf16[192,3072]{1,0:T(8,128)(2,1)S(1)}, bf16[192,3072]{1,0:T(8,128)(2,1)}, u32[]{:S(2)}) copy-start(bf16[192,3072]{1,0:T(8,128)(2,1)} %param.27) | copy-start | bytes 3538948
  77.4 6.2 %copy-start.1 = (bf16[768,768]{1,0:T(8,128)(2,1)S(1)}, bf16[768,768]{1,0:T(8,128)(2,1)}, u32[]{:S(2)}) copy-start(bf16[768,768]{1,0:T(8,128)(2,1)} %param.29) | copy-start | bytes 3538948
  312.3 99.7 %copy-start.10 = (f32[4,1,192]{2,0,1:T(4,128)S(1)}, f32[4,1,192]{2,0,1:T(4,128)}, u32[]{:S(2)}) copy-start(f32[4,1,192]{2,0,1:T(4,128)} %get-tuple-element.137) | copy-start | bytes 9220
  312.3 100.4 %copy-start.9 = (f32[2,8,768]{2,1,0:T(8,128)S(1)}, f32[2,8,768]{2,1,0:T(8,128)}, u32[]{:S(2)}) copy-start(f32[2,8,768]{2,1,0:T(8,128)} %get-tuple-element.101) | copy-start | bytes 147460
  312.4 100.6 %copy-start.12 = (f32[2,768]{1,0:T(2,128)S(1)}, f32[2,768]{1,0:T(2,128)}, u32[]{:S(2)}) copy-start(f32[2,768]{1,0:T(2,128)} %get-tuple-element.102) | copy-start | bytes 18436
  312.4 100.6 %copy-start.13 = (f32[2,768]{1,0:T(2,128)S(1)}, f32[2,768]{1,0:T(2,128)}, u32[]{:S(2)}) copy-start(f32[2,768]{1,0:T(2,128)} %get-tuple-element.103) | copy-start | bytes 18436
  312.4 100.6 %copy-start.14 = (f32[2,768]{1,0:T(2,128)S(1)}, f32[2,768]{1,0:T(2,128)}, u32[]{:S(2)}) copy-start(f32[2,768]{1,0:T(2,128)} %get-tuple-element.104) | copy-start | bytes 18436
  312.4 100.5 %copy-start.15 = (f32[2,768]{1,0:T(2,128)S(1)}, f32[2,768]{1,0:T(2,128)}, u32[]{:S(2)}) copy-start(f32[2,768]{1,0:T(2,128)} %get-tuple-element.105) | copy-start | bytes 18436
  312.4 102.0 %copy-start.16 = (f32[1,1024]{1,0:T(1,128)S(1)}, f32[1,1024]{1,0:T(1,128)}, u32[]{:S(2)}) copy-start(f32[1,1024]{1,0:T(1,128)} %get-tuple-element.106) | copy-start | bytes 12292
  312.4 102.0 %copy-start.17 = (f32[1,1024]{1,0:T(1,128)S(1)}, f32[1,1024]{1,0:T(1,128)}, u32[]{:S(2)}) copy-start(f32[1,1024]{1,0:T(1,128)} %get-tuple-element.107) | copy-start | bytes 12292
  312.4 102.0 %copy-start.18 = (f32[1,1024]{1,0:T(1,128)S(1)}, f32[1,1024]{1,0:T(1,128)}, u32[]{:S(2)}) copy-start(f32[1,1024]{1,0:T(1,128)} %get-tuple-element.108) | copy-start | bytes 12292
  488.5 5.3 %copy-start.8 = (bf16[192,768]{1,0:T(8,128)(2,1)S(1)}, bf16[192,768]{1,0:T(8,128)(2,1)}, u32[]{:S(2)}) copy-start(bf16[192,768]{1,0:T(8,128)(2,1)} %get-tuple-element.120) | copy-start | bytes 884740
  491.2 3.4 copy-start.7
  491.2 5.0 copy-start.6
  493.8 4.1 copy-start.5
  503.5 2.9 copy-start.11
  503.5 3.5 copy-start.4
  507.0 2.8 copy-start
  511.5 6.0 %copy-start.3 = (f32[128,1152]{1,0:T(8,128)S(1)}, f32[128,1152]{1,0:T(8,128)}, u32[]{:S(2)}) copy-start(f32[128,1152]{1,0:T(8,128)} %get-tuple-element.184) | copy-start | bytes 1769476
